TPU v7x, 32 devices: a whole 2x2x4 slice. The times are simulated.
32 devices in a mesh: orb: 8 (over z, core), aux: 4 (over y, x).
Axes of the slice: x: 2, y: 2, z: 4, core: 2. Of those that a mesh axis runs over, the one named last changes fastest.
Arguments:
- three_center: bfloat16 [128, 128, 128, 128], P(('orb', 'aux')), may hold values from -0.5 to 0.5
- screening: int32 [128, 3], P(('orb', 'aux')), may hold values from -1 to 255, as said below
- density_factor: bfloat16 [32768, 128], P('orb'), may hold values from -0.23925781 to 0.23925781
- metric_inverse: bfloat16 [512, 512], replicated, may hold values from -1 to 1, as said below
Outputs:
- exchange_block: bfloat16 [1024, 256], P('orb')
Inputs may be any that keep to these rules, and one draw needn't show every extreme that they name: `screening`: A device's slots are 4 consecutive rows, devices in order of orb index then aux index. Column 0 equals the orb index and column 2 the aux index of the device holding the row. Column 1 is an orbital block, or -1 for an empty slot; empty slots follow the live ones, the live orbital blocks of a device are distinct, every device has 1 to 4 live slots, and some device has 4. `metric_inverse`: Symmetric.
All inputs are finite; a program needn't handle non-finite values.
Results may differ from a plain program's by a relative error of at most 0.0063.
Values may be sent and summed in bfloat16 or wider, within the bound.
No kernel may reach another device: no remote copies, remote signals or barrier semaphores. Data moves between devices by JAX's collectives and lax.ppermute only.
A program may use at most 128 MiB of HBM per device.

v0:
```python
import jax
import jax.numpy as jnp
from jax import lax
from jax.sharding import PartitionSpec as P


def from_behind(x, axis, by):
    length = lax.axis_size(axis)
    return lax.ppermute(x, axis, [(i, (i + by) % length) for i in range(length)])


def keep_same(current):
    return current


def contract_arrived(three_center, orbitals, arrived, running):
    slot_count = three_center.shape[0]

    def one_slot(slot_index, carried):
        inside = orbitals[slot_index] >= 0

        def add_tile(current):
            row_block = lax.dynamic_index_in_dim(arrived, slot_index, 0, keepdims=False)
            tile_now = lax.dynamic_index_in_dim(three_center, slot_index, 0, keepdims=False)
            return current + jnp.einsum(
                "mlp,li->mip", tile_now, row_block, preferred_element_type=jnp.float32
            )

        return lax.cond(inside, add_tile, keep_same, carried)

    return lax.fori_loop(0, slot_count, one_slot, running)


def on_device(three_center, screening, density_factor, metric_inverse):
    block_width = three_center.shape[1]
    slot_count = three_center.shape[0]
    occupied = density_factor.shape[1]
    orbitals = screening[:, 1]
    zero_start = jnp.zeros((block_width, occupied, block_width), jnp.float32)
    wanted_all = lax.all_gather(orbitals, "orb", axis=0, tiled=True)
    owned_count = density_factor.shape[0] // block_width
    local_index = wanted_all - lax.axis_index("orb") * owned_count
    owned_here = (wanted_all >= 0) & (local_index >= 0) & (local_index < owned_count)
    blocks_here = density_factor.reshape(owned_count, block_width, occupied)
    picked = blocks_here[jnp.clip(local_index, 0, owned_count - 1)]
    picked = jnp.where(owned_here[:, None, None], picked, jnp.zeros_like(picked))
    orb_count = lax.axis_size("orb")
    picked = picked.reshape(orb_count, slot_count * block_width, occupied)
    arrived = lax.all_to_all(picked, "orb", split_axis=0, concat_axis=0, tiled=True)
    arrived = arrived.reshape(orb_count, slot_count, block_width, occupied)
    owner_index = jnp.clip(orbitals // owned_count, 0, orb_count - 1)
    slot_ids = jnp.arange(slot_count, dtype=jnp.int32)
    arrived = arrived[owner_index, slot_ids]
    partial_half = contract_arrived(three_center, orbitals, arrived, zero_start)
    half_local = partial_half.astype(jnp.bfloat16)
    relaid = lax.all_to_all(half_local, "aux", split_axis=1, concat_axis=2, tiled=True)
    fitted_part = jnp.einsum(
        "miP,PQ->miQ", relaid, metric_inverse, preferred_element_type=jnp.float32
    )
    fitted = fitted_part.astype(jnp.bfloat16)
    following = from_behind(relaid, "orb", -1)
    diagonal = jnp.einsum("miq,niq->mn", fitted, relaid, preferred_element_type=jnp.float32)
    coupling = jnp.einsum("miq,niq->mn", fitted, following, preferred_element_type=jnp.float32)
    summed = lax.psum(jnp.concatenate([diagonal, coupling], axis=1), "aux")
    return summed.astype(jnp.bfloat16)


def solution(mesh):
    placed = (P(("orb", "aux"), None, None, None), P(("orb", "aux"), None), P("orb", None), P())
    return jax.shard_map(
        on_device, mesh=mesh, in_specs=placed, out_specs=P("orb", None), check_vma=False
    )
```

profile of v0, /device:TPU:0, one launch (start us, length us, event | category | flops | bytes accessed | tf_op | source)
XLA Modules:
  0.0 229.8 jit_solution(11306803369627517061)
XLA Ops:
  0.0 1.0 or_reduce_fusion
  1.0 1.3 dynamic-slice
  3.3 10.6 %all-reduce = s32[32]{0:T(128)S(1)} all-reduce(s32[32]{0:T(128)S(1)} %dynamic-update-slice), channel_id=2, replica_groups=mesh['orb'=8,'aux'=4] {'orb'}, use_global_device_ids=true, to_apply=%add | all-reduce | flops 32 | bytes 256
  14.2 0.8 gather_fusion
  15.0 0.7 bitcast_select_fusion
  15.7 29.0 %all_to_all.23 = bf16[8,512,128]{2,1,0:T(8,128)(2,1)S(1)} all-to-all(bf16[8,512,128]{2,1,0:T(8,128)(2,1)S(1)} %bitcast_select_fusion), channel_id=1, replica_groups=mesh['orb'=8,'aux'=4] {'orb'}, dimensions={0} | all-to-all | bytes 2097152 | tf_op jit(solution)/shard_map/all_to_all | solution.py:49
  44.7 0.6 gather_fusion.1
  45.4 4.3 %broadcast_in_dim.26 = f32[128,128,128]{2,1,0:T(8,128)} broadcast(f32[]{:T(128)} %constant.60.clone.1), dimensions={} | broadcast | bytes 8388612 | tf_op jit(solution)/shard_map/broadcast_in_dim | solution.py:39
  49.7 22.9 %while.16 = (s32[]{:T(128)}, f32[128,128,128]{2,1,0:T(8,128)}, s32[4]{0:T(128)S(1)}, bf16[4,128,128]{1,2,0:T(8,128)(2,1)S(1)}, bf16[4,128,128,128]{3,2,1,0:T(8,128)(2,1)}, /*index=5*/s32[]{:T(128)}, s32[1]{0:T(128)}) while((s32[]{:T(128)}, f32[128,128,128]{2,1,0:T(8,128)}, s32[4]{0:T(128)S(1)}, bf16[4,128,128]{1,2,0:T(8,128)(2,1)S(1)}, ...), condition=%wide.region_3.4_spmd, body=%wide.region_0.3_spmd.sunk | while | flops 538968064 | bytes 21005488 | solution.py:31
  50.8 9.2 %conditional.2 = (f32[128,128,128]{2,1,0:T(8,128)}) conditional(s32[]{:T(128)} %bitcast.39, f32[128,128,128]{2,1,0:T(8,128)} %get-tuple-element.181, (s32[]{:T(128)}, bf16[4,128,128]{1,2,0:T(8,128)(2,1)S(1)}, bf16[4,128,128,128]{3,2,1,0:T(8,128)(2,1)}, f32[128,128,128]{2,1,0:T(8,128)}) %tuple.42), branch_computations={%region_1.1_spmd, %region_2.2_spmd} | conditional | flops 538968064 | bytes 21005354 | solution.py:29
  50.8 9.1 %bitcast_add_fusion = f32[128,128,128]{2,1,0:T(8,128)} fusion(f32[128,128,128]{2,1,0:T(8,128)} %get-tuple-element.108, bf16[4,128,128,128]{3,2,1,0:T(8,128)(2,1)} %get-tuple-element.111, s32[]{:T(128)S(6)} %select_n.25, bf16[4,128,128]{1,2,0:T(8,128)(2,1)S(1)} %get-tuple-element.109), kind=kOutput, calls=%fused_computation.2 | convolution fusion | flops 538968064 | bytes 21005312 | tf_op jit(solution)/shard_map/while/body/eval_jaxpr/cond/branch_1_fun/mlp,li->mip/dot_general | solution.py:25
  61.1 9.2 %conditional.2 = (f32[128,128,128]{2,1,0:T(8,128)}) conditional(s32[]{:T(128)} %bitcast.39, f32[128,128,128]{2,1,0:T(8,128)} %get-tuple-element.181, (s32[]{:T(128)}, bf16[4,128,128]{1,2,0:T(8,128)(2,1)S(1)}, bf16[4,128,128,128]{3,2,1,0:T(8,128)(2,1)}, f32[128,128,128]{2,1,0:T(8,128)}) %tuple.42), branch_computations={%region_1.1_spmd, %region_2.2_spmd} | conditional | flops 538968064 | bytes 21005354 | solution.py:29
  61.1 9.1 %bitcast_add_fusion = f32[128,128,128]{2,1,0:T(8,128)} fusion(f32[128,128,128]{2,1,0:T(8,128)} %get-tuple-element.108, bf16[4,128,128,128]{3,2,1,0:T(8,128)(2,1)} %get-tuple-element.111, s32[]{:T(128)S(6)} %select_n.25, bf16[4,128,128]{1,2,0:T(8,128)(2,1)S(1)} %get-tuple-element.109), kind=kOutput, calls=%fused_computation.2 | convolution fusion | flops 538968064 | bytes 21005312 | tf_op jit(solution)/shard_map/while/body/eval_jaxpr/cond/branch_1_fun/mlp,li->mip/dot_general | solution.py:25
  72.6 8.2 %copy.19 = bf16[128,128,128]{2,0,1:T(8,128)(2,1)S(1)} copy(f32[128,128,128]{2,1,0:T(8,128)} %get-tuple-element.119) | data formatting | bytes 12582912 | tf_op jit(solution)/shard_map/while | solution.py:31
  80.8 37.0 %all_to_all.24 = bf16[128,128,128]{2,0,1:T(8,128)(2,1)S(1)} all-to-all(bf16[128,128,128]{2,0,1:T(8,128)(2,1)S(1)} %copy.19), channel_id=1, replica_groups=mesh['orb'=8,'aux'=4] {'aux'}, dimensions={1} | all-to-all | bytes 8388608 | tf_op jit(solution)/shard_map/all_to_all | solution.py:56
  117.8 5.9 %copy.20 = bf16[128,4,32,128]{3,1,0,2:T(4,128)(2,1)} copy(bf16[128,4,32,128]{3,0,2,1:T(8,128)(2,1)S(1)} %bitcast.41) | data formatting | bytes 8388608 | tf_op jit(solution)/shard_map/all_to_all | solution.py:56
  123.7 7.3 %all_to_all.20 = bf16[128,32,512]{2,0,1:T(8,128)(2,1)} reshape(bf16[128,32,4,128]{3,2,0,1:T(4,128)(2,1)} %bitcast.42) | data formatting | bytes 8388608 | tf_op jit(solution)/shard_map/all_to_all | solution.py:56
  130.9 33.2 %collective-permute-start = (bf16[128,32,512]{2,0,1:T(8,128)(2,1)}, bf16[128,32,512]{2,0,1:T(8,128)(2,1)S(1)}, u32[]{:S(2)}, u32[]{:S(2)}) collective-permute-start(bf16[128,32,512]{2,0,1:T(8,128)(2,1)} %all_to_all.20), channel_id=1, source_target_pairs={{0,28},{4,0},{8,4},{12,8},{16,12},{20,16},{24,20},{28,24},{1,29},{... | collective-permute-start | bytes 12582920 | tf_op jit(solution)/shard_map/ppermute | solution.py:9
  164.2 4.6 %convolution_convert_fusion = bf16[128,32,512]{2,0,1:T(8,128)(2,1)S(1)} fusion(bf16[128,32,512]{2,0,1:T(8,128)(2,1)} %all_to_all.20, bf16[512,512]{1,0:T(8,128)(2,1)S(1)} %copy-done.2), kind=kOutput, calls=%fused_computation.11 | convolution fusion | flops 2149580800 | bytes 8912896 | tf_op jit(solution)/shard_map/miP,PQ->miQ/dot_general | solution.py:57
  168.7 1.2 convolution_bitcast_fusion.1
  170.0 40.5 %collective-permute-done = bf16[128,32,512]{2,0,1:T(8,128)(2,1)S(1)} collective-permute-done((bf16[128,32,512]{2,0,1:T(8,128)(2,1)}, bf16[128,32,512]{2,0,1:T(8,128)(2,1)S(1)}, u32[]{:S(2)}, u32[]{:S(2)}) %collective-permute-start) | collective-permute-done | bytes 4194336 | tf_op jit(solution)/shard_map/ppermute | solution.py:9
  210.5 1.2 convolution_bitcast_fusion
  211.8 17.3 %all-reduce.2 = bf16[128,256]{0,1:T(8,128)(2,1)S(1)} all-reduce(f32[128,256]{0,1:T(8,128)S(1)} %pad_maximum_fusion), channel_id=1, replica_groups=mesh['orb'=8,'aux'=4] {'aux'}, use_global_device_ids=true, to_apply=%region_4.5 | all-reduce | flops 32768 | bytes 196608 | tf_op jit(solution)/shard_map/psum | solution.py:64
  229.1 0.7 copy.16
  (22 shorter events, 2.9 us)
Async XLA Ops:
  0.0 14.2 %copy-start = (bf16[4096,128]{1,0:T(8,128)(2,1)S(1)}, bf16[4096,128]{1,0:T(8,128)(2,1)}, u32[]{:S(2)}) copy-start(bf16[4096,128]{1,0:T(8,128)(2,1)} %param.10) | copy-start | bytes 3145732
  123.7 40.5 %copy-start.2 = (bf16[512,512]{1,0:T(8,128)(2,1)S(1)}, bf16[512,512]{1,0:T(8,128)(2,1)}, u32[]{:S(2)}) copy-start(bf16[512,512]{1,0:T(8,128)(2,1)} %param.11) | copy-start | bytes 1572868
  130.9 37.8 %copy-start.1 = (bf16[128,32,512]{2,0,1:T(8,128)(2,1)S(1)}, bf16[128,32,512]{2,0,1:T(8,128)(2,1)}, u32[]{:S(2)}) copy-start(bf16[128,32,512]{2,0,1:T(8,128)(2,1)} %all_to_all.20) | copy-start | bytes 12582916
  130.9 79.6 %collective-permute-start = (bf16[128,32,512]{2,0,1:T(8,128)(2,1)}, bf16[128,32,512]{2,0,1:T(8,128)(2,1)S(1)}, u32[]{:S(2)}, u32[]{:S(2)}) collective-permute-start(bf16[128,32,512]{2,0,1:T(8,128)(2,1)} %all_to_all.20), channel_id=1, source_target_pairs={{0,28},{4,0},{8,4},{12,8},{16,12},{20,16},{24,20},{28,24},{1,29},{... | collective-permute-start | bytes 12582920 | tf_op jit(solution)/shard_map/ppermute | solution.py:9
where the time goes:
time: 230 us
  blocking collectives  93.9 us (41%)
  waiting for transfers between devices  40.5 us (18%)
  starting transfers between devices  33.2 us (14%)
  local copies, waits for them, and re-layouts  31.9 us (14%)
  matrix products  25.3 us (11%)
  loops' own time  2.4 us (1%)
    ppermute x1, waiting for transfers between devices, from_behind(): lax.ppermute(x, axis, [(i, (i + by) % length) for i in range(length)])  40.5 us
    all_to_all x1, blocking collectives, on_device(): lax.all_to_all(half_local, 'aux', split_axis=1, concat_axis=2, tiled=True)  37 us
    ppermute x1, starting transfers between devices, from_behind(): lax.ppermute(x, axis, [(i, (i + by) % length) for i in range(length)])  33.2 us
    all_to_all x1, blocking collectives, on_device(): lax.all_to_all(picked, 'orb', split_axis=0, concat_axis=0, tiled=True)  29 us
    dot_general x2, matrix products, add_tile(): jnp.einsum('mlp,li->mip', tile_now, row_block, preferred_element_type=jnp...  18.3 us
    psum x1, blocking collectives, on_device(): summed = lax.psum(jnp.concatenate([diagonal, coupling], axis=1), 'aux')  17.3 us
    all_to_all x2, local copies, waits for them, and re-layouts, on_device(): lax.all_to_all(half_local, 'aux', split_axis=1, concat_axis=2, tiled=True)  13.1 us
    unnamed x1, blocking collectives  10.6 us
  transfers between devices with their start and end apart: 1, of which 1 were waited for; matrix products, arithmetic and copies ran while one was open for 3% of the time, Pallas kernels for 0%

commit v1 on v0

v1 whole, which is shorter than its diff:
```python
import functools

import jax
import jax.numpy as jnp
from jax import lax
from jax.experimental import pallas as pl
from jax.experimental.pallas import tpu as pltpu
from jax.sharding import PartitionSpec as P


PARTS = (1, 1)
STEP_ROWS = 16
GROUP = 4
VMEM = pltpu.VMEM
SMEM_SPEC = pl.BlockSpec(memory_space=pltpu.SMEM)
VMEM_SPEC = pl.BlockSpec(memory_space=pltpu.VMEM)


def local_call(kernel, out_shape, operands, scalars, flops, scratch=()):
    operands = [pltpu.with_memory_space_constraint(x, VMEM) for x in operands]
    out_shape = jax.tree.map(lambda x: VMEM(x.shape, x.dtype), out_shape)
    return pl.pallas_call(
        kernel,
        out_shape=out_shape,
        in_specs=[SMEM_SPEC] * len(scalars) + [VMEM_SPEC] * len(operands),
        out_specs=jax.tree.map(lambda _: VMEM_SPEC, out_shape),
        scratch_shapes=list(scratch),
        cost_estimate=pl.CostEstimate(flops=flops, bytes_accessed=1 << 20, transcendentals=0),
        compiler_params=pltpu.CompilerParams(vmem_limit_bytes=12 << 20),
    )(*scalars, *operands)


def load_kernel(first, source_ref, loaded_ref, sems):
    copies = [
        pltpu.make_async_copy(source_ref.at[first + slot], loaded_ref.at[slot], sems.at[slot])
        for slot in range(loaded_ref.shape[0])
    ]
    for copy in copies:
        copy.start()
    for copy in copies:
        copy.wait()


def load(source, first, count):
    return pl.pallas_call(
        functools.partial(load_kernel, first),
        out_shape=VMEM((count, *source.shape[1:]), source.dtype),
        in_specs=[pl.BlockSpec(memory_space=pl.ANY)],
        out_specs=VMEM_SPEC,
        scratch_shapes=[pltpu.SemaphoreType.DMA((count,))],
        cost_estimate=pl.CostEstimate(
            flops=0, bytes_accessed=count * source[0].size * source.dtype.itemsize, transcendentals=0
        ),
        compiler_params=pltpu.CompilerParams(vmem_limit_bytes=1 << 20),
        name="load",
    )(source)


def pick_kernel(owned, block, slot_count, aux_count, chunk_rows, *refs):
    dest_count = (len(refs) - 4) // (1 + len(chunk_rows))
    place_ref = refs[0]
    wanted = refs[1 : 1 + dest_count]
    own_ref, partner_ref = refs[1 + dest_count : 3 + dest_count]
    given = refs[3 + dest_count : -1]
    turned = refs[-1]
    base, core, me = place_ref[0], place_ref[1], place_ref[2]
    share = turned.shape[0] // aux_count
    for dest in range(dest_count):
        for slot in range(slot_count):
            orbital = wanted[dest][slot, 1]
            local = orbital - base
            inside = (orbital >= 0) & (local >= 0) & (local < 2 * owned)
            upper = jnp.where(local >= owned, 1, 0)
            row = jnp.clip(local - upper * owned, 0, owned - 1) * block
            rows = pl.ds(pl.multiple_of(row, block), block)
            picked = jnp.where(
                upper == core, own_ref[rows, :].astype(jnp.float32), partner_ref[rows, :].astype(jnp.float32)
            )
            picked = jnp.where(inside, picked, jnp.zeros_like(picked))
            turned[...] = picked.T
            for away in range(aux_count):
                start = pl.multiple_of((me ^ away) * share, share)
                first = 0
                for chunk, count in enumerate(chunk_rows):
                    given[dest * len(chunk_rows) + chunk][slot, away * count : (away + 1) * count, :] = turned[
                        pl.ds(start + first, count), :
                    ].astype(jnp.bfloat16)
                    first += count


def half_kernel(aux_count, tile_count, *refs):
    tiles = refs[:tile_count]
    parts = refs[tile_count : -1 - aux_count]
    outs = refs[-1 - aux_count : -1]
    wide = refs[-1]
    slot_count, block = parts[0].shape[0], tiles[0].shape[1]
    width = parts[0].shape[1]
    count = width // aux_count
    rows = STEP_ROWS
    stride = rows + 1
    columns = []
    for slot in range(slot_count):
        total = parts[0][slot].astype(jnp.float32)
        for part in parts[1:]:
            total = total + part[slot].astype(jnp.float32)
        columns.append(total.astype(jnp.bfloat16))
    left = jnp.concatenate(columns, axis=1)

    def step(index, carry):
        base = pl.multiple_of(index * rows, rows)
        for row in range(0, rows, 2):
            right = jnp.concatenate(
                [
                    jnp.concatenate(
                        [tile[:, base + row + m].reshape(-1, block) for tile in tiles], axis=0
                    )
                    for m in range(2)
                ],
                axis=1,
            )
            product = jnp.dot(left, right, preferred_element_type=jnp.float32)
            wide[pl.ds(row, width, stride=stride), :] = product[:, :block]
            wide[pl.ds(row + 1, width, stride=stride), :] = product[:, block:]
        for away in range(aux_count):
            for i in range(count):
                outs[away][i, pl.ds(base, rows), :] = wide[
                    pl.ds((away * count + i) * stride, rows), :
                ].astype(jnp.bfloat16)
        return carry

    lax.fori_loop(0, block // rows, step, 0)


def gram(left_ref, right_parts):
    count = left_ref.shape[0]
    left = jnp.concatenate([left_ref[i] for i in range(count)], axis=1)
    right = jnp.concatenate([part[i] for i in range(count) for part in right_parts], axis=1)
    return lax.dot_general(left, right, (((1,), (1,)), ((), ())), preferred_element_type=jnp.float32)


def fit_kernel(aux_count, *refs):
    place_ref, metric_ref = refs[:2]
    parts = refs[2 : 2 + aux_count]
    before = refs[2 + aux_count : -3]
    fitted_ref, after_ref, turned = refs[-3:]
    count, block, width = parts[0].shape
    me = place_ref[2]
    for row in range(aux_count):
        for column in range(aux_count):
            turned[row * width : (row + 1) * width, column * width : (column + 1) * width] = metric_ref[
                pl.ds(pl.multiple_of((me ^ row) * width, width), width),
                pl.ds(pl.multiple_of((me ^ column) * width, width), width),
            ]
    metric = turned[...]
    for first in range(0, count, GROUP):
        here = min(GROUP, count - first)
        half = jnp.concatenate(
            [part[first : first + here].reshape(here * block, width) for part in parts], axis=1
        )
        fitted = jnp.dot(half, metric, preferred_element_type=jnp.float32).astype(jnp.bfloat16)
        fitted_ref[first : first + here] = fitted.reshape(here, block, aux_count * width)
    total = gram(fitted_ref, parts)
    for ref in before:
        total = total + ref[...]
    after_ref[...] = total


def couple_kernel(aux_count, *refs):
    total = gram(refs[0], refs[1 : 1 + aux_count])
    for ref in refs[1 + aux_count : -1]:
        total = total + ref[...]
    refs[-1][...] = total


def on_device(orb_count, aux_count, three_center, screening, density_factor, metric_inverse):
    slot_count, block = three_center.shape[:2]
    occupied = density_factor.shape[1]
    owned = density_factor.shape[0] // block
    share = occupied // aux_count
    chunk_rows = [share * part // sum(PARTS) for part in PARTS]
    chunks = len(chunk_rows)
    bf16, f32 = jnp.bfloat16, jnp.float32

    orb = lax.axis_index("orb")
    aux = lax.axis_index("aux")
    place = jnp.stack([(orb >> 1) * (2 * owned), orb & 1, aux]).astype(jnp.int32)

    def along_orb(x, by):
        return lax.ppermute(x, "orb", [(i, (i + by) % orb_count) for i in range(orb_count)])

    def across_aux(x, away):
        return lax.ppermute(x, "aux", [(i, i ^ away) for i in range(aux_count)])

    loads = []
    for number in range(2):
        loads.append(load(three_center, number * (slot_count // 2), slot_count // 2))
    partner = lax.ppermute(density_factor, "orb", [(i, i ^ 1) for i in range(orb_count)])
    shifts = list(range(2, orb_count, 2))
    wanted = [screening]
    for by in shifts:
        wanted.append(along_orb(screening, by))
    given = local_call(
        functools.partial(pick_kernel, owned, block, slot_count, aux_count, chunk_rows),
        [jax.ShapeDtypeStruct((slot_count, aux_count * count, block), bf16) for _ in wanted for count in chunk_rows],
        [density_factor, partner],
        [place, *wanted],
        0,
        [pltpu.VMEM((occupied, block), f32)],
    )
    here, following = [], []
    for c, count in enumerate(chunk_rows):
        arrived = [given[c]]
        for dest, by in enumerate(shifts, 1):
            arrived.append(along_orb(given[dest * chunks + c], -by))
        halves = local_call(
            functools.partial(half_kernel, aux_count, len(loads)),
            [jax.ShapeDtypeStruct((count, block, block), bf16)] * aux_count,
            [*loads, *arrived],
            [],
            2 * slot_count * block**3 * count * aux_count,
            [pltpu.VMEM((aux_count * count * (STEP_ROWS + 1), block), f32)],
        )
        mine, theirs = [halves[0]], []
        for away in range(1, aux_count):
            mine.append(across_aux(halves[away], away))
        for away in range(aux_count):
            theirs.append(along_orb(mine[away], -1))
        here.append(mine)
        following.append(theirs)

    diagonal, coupling = [], []
    width = aux_count * block
    for c, count in enumerate(chunk_rows):
        fitted, *diagonal = local_call(
            functools.partial(fit_kernel, aux_count),
            [
                jax.ShapeDtypeStruct((count, block, width), bf16),
                jax.ShapeDtypeStruct((block, block), f32),
            ],
            [metric_inverse, *here[c], *diagonal],
            [place],
            2 * count * block * width * (width + block),
            [pltpu.VMEM((width, width), bf16)],
        )
        coupling = [
            local_call(
                functools.partial(couple_kernel, aux_count),
                jax.ShapeDtypeStruct((block, block), f32),
                [fitted, *following[c], *coupling],
                [],
                2 * count * block * width * block,
            )
        ]

    def sum_aux(x):
        terms = {}
        for away in reversed(range(1, aux_count)):
            terms[away] = across_aux(x, away)
        terms = [x] + [terms[away] for away in range(1, aux_count)]
        while len(terms) > 1:
            terms = [a + b for a, b in zip(terms[::2], terms[1::2])]
        return terms[0].astype(bf16)

    return jnp.concatenate([sum_aux(diagonal[0]), sum_aux(coupling[0])], axis=1)


def solution(mesh):
    placed = (P(("orb", "aux"), None, None, None), P(("orb", "aux"), None), P("orb", None), P())
    sizes = mesh.shape["orb"], mesh.shape["aux"]

    def body(*args):
        return on_device(*sizes, *args)

    return jax.shard_map(body, mesh=mesh, in_specs=placed, out_specs=P("orb", None), check_vma=False)
```

time: 230 us -> 116 us (0.50)
  blocking collectives: 93.9 us -> 0 us
  matrix products: 25.3 us -> 0 us
  local copies, waits for them, and re-layouts: 31.9 us -> 7.68 us
  Pallas kernels: 0 us -> 17.1 us
  waiting for transfers between devices: 40.5 us -> 50.8 us
  starting transfers between devices: 33.2 us -> 38.7 us
  loops' own time: 2.4 us -> 0 us
    all_to_all x2 -> x0, blocking collectives: 66 us -> none  [the longest x1 37 us: on_device(): lax.all_to_all(half_local, 'aux', split_axis=1, concat_axis=2, tiled=True)]
    dot_general x5 -> x0, matrix products: 25.3 us -> none  [the longest x2 18.3 us: add_tile(): jnp.einsum('mlp,li->mip', tile_now, row_block, preferred_element_type=jnp...]
    psum x1 -> x0, blocking collectives: 17.3 us -> none  [on_device(): summed = lax.psum(jnp.concatenate([diagonal, coupling], axis=1), 'aux')]
    pallas_call x0 -> x9, Pallas kernels: none -> 17.1 us  [the longest x7 16 us: local_call(): pl.pallas_call(kernel, out_shape=out_shape, in_specs=[SMEM_SPEC] * len(sc...]
    all_to_all x2 -> x0, local copies, waits for them, and re-layouts: 13.1 us -> none  [on_device(): lax.all_to_all(half_local, 'aux', split_axis=1, concat_axis=2, tiled=True)]
    unnamed x1 -> x0, blocking collectives: 10.6 us -> none
    ppermute x1 -> x30, waiting for transfers between devices: 40.5 us -> 50.8 us  [the longest x12 32.2 us: across_aux(): return lax.ppermute(x, 'aux', [(i, i ^ away) for i in range(aux_count)])]
    while x2 -> x0, local copies, waits for them, and re-layouts: 8.37 us -> none  [contract_arrived(): return lax.fori_loop(0, slot_count, one_slot, running)]
  transfers between devices with their start and end apart: 1 -> 30, of which waited for: 1 -> 12; matrix products, arithmetic and copies ran while one was open for 3% -> 0% of each run, Pallas kernels for 0% -> 14%
where the time goes in v1:
time: 116 us; the launch traced here: 115 us
  waiting for transfers between devices  50.8 us (44%)
  starting transfers between devices  38.7 us (33%)
  Pallas kernels  17.1 us (15%)
  local copies, waits for them, and re-layouts  7.68 us (7%)
    ppermute x12, waiting for transfers between devices, across_aux(): return lax.ppermute(x, 'aux', [(i, i ^ away) for i in range(aux_count)])  32.2 us
    ppermute x17, starting transfers between devices, along_orb(): lax.ppermute(x, 'orb', [(i, (i + by) % orb_count) for i in range(orb_coun...  22.5 us
    ppermute x17, waiting for transfers between devices, along_orb(): lax.ppermute(x, 'orb', [(i, (i + by) % orb_count) for i in range(orb_coun...  18.6 us
    pallas_call x7, Pallas kernels, local_call(): pl.pallas_call(kernel, out_shape=out_shape, in_specs=[SMEM_SPEC] * len(sc...  16 us
    ppermute x12, starting transfers between devices, across_aux(): return lax.ppermute(x, 'aux', [(i, i ^ away) for i in range(aux_count)])  15.8 us
    unnamed x8, local copies, waits for them, and re-layouts  7.68 us
  transfers between devices with their start and end apart: 30, of which 12 were waited for; matrix products, arithmetic and copies ran while one was open for 0% of the time, Pallas kernels for 14%

profile of v1, /device:TPU:0, one launch (start us, length us, event | category | flops | bytes accessed | tf_op | source)
XLA Modules:
  0.0 115.2 jit_solution(4749759780370623340)
XLA Ops:
  0.5 2.6 %collective-permute-start = (s32[4,3]{1,0:T(4,128)}, s32[4,3]{1,0:T(4,128)S(1)}, u32[]{:S(2)}, u32[]{:S(2)}) collective-permute-start(s32[4,3]{1,0:T(4,128)} %refs_1_.3), channel_id=1, source_target_pairs={{0,8},{4,12},{8,16},{12,20},{16,24},{20,28},{24,0},{28,4},{1,9},{5... | collective-permute-start | bytes 152 | tf_op jit(solution)/shard_map/ppermute | solution.py:189
  3.1 2.6 %collective-permute-start.1 = (s32[4,3]{1,0:T(4,128)}, s32[4,3]{1,0:T(4,128)S(1)}, u32[]{:S(2)}, u32[]{:S(2)}) collective-permute-start(s32[4,3]{1,0:T(4,128)} %refs_1_.3), channel_id=1, source_target_pairs={{0,16},{4,20},{8,24},{12,28},{16,0},{20,4},{24,8},{28,12},{1,17},{... | collective-permute-start | bytes 152 | tf_op jit(solution)/shard_map/ppermute | solution.py:189
  7.8 1.7 %collective-permute-done.2.refs_4_ = s32[4,3]{1,0:T(4,128)S(1)} collective-permute-done((s32[4,3]{1,0:T(4,128)}, s32[4,3]{1,0:T(4,128)S(1)}, u32[]{:S(2)}, u32[]{:S(2)}) %collective-permute-start.2) | collective-permute-done | bytes 80 | tf_op jit(solution)/shard_map/ppermute | solution.py:189
  12.4 3.2 %collective-permute-start.4 = (bf16[4,64,128]{2,1,0:T(8,128)(2,1)S(1)}, bf16[4,64,128]{2,1,0:T(8,128)(2,1)S(1)}, u32[]{:S(2)}, u32[]{:S(2)}) collective-permute-start(bf16[4,64,128]{2,1,0:T(8,128)(2,1)S(1)} %get-tuple-element.26), channel_id=1, source_target_pairs={{0,24},{4,28},{8,0},{12,4},{16,8},{20,12},{24,16},{28,20},{1,25},{... | collective-permute-start | bytes 196616 | tf_op jit(solution)/shard_map/ppermute | solution.py:189
  16.2 5.8 %copy-done = bf16[4,128,128,128]{3,2,1,0:T(8,128)(2,1)S(1)} copy-done((bf16[4,128,128,128]{3,2,1,0:T(8,128)(2,1)S(1)}, bf16[4,128,128,128]{3,2,1,0:T(8,128)(2,1)}, u32[]{:S(2)}) %copy-start) | copy-done | bytes 16777240
  23.1 3.2 %collective-permute-start.10 = (bf16[4,64,128]{2,1,0:T(8,128)(2,1)S(1)}, bf16[4,64,128]{2,1,0:T(8,128)(2,1)S(1)}, u32[]{:S(2)}, u32[]{:S(2)}) collective-permute-start(bf16[4,64,128]{2,1,0:T(8,128)(2,1)S(1)} %get-tuple-element.34), channel_id=1, source_target_pairs={{0,24},{4,28},{8,0},{12,4},{16,8},{20,12},{24,16},{28,20},{1,25},{... | collective-permute-start | bytes 196616 | tf_op jit(solution)/shard_map/ppermute | solution.py:189
  27.5 4.1 %shard_map.47 = (bf16[16,128,128]{2,1,0:T(8,128)(2,1)S(1)}, bf16[16,128,128]{2,1,0:T(8,128)(2,1)S(1)}, bf16[16,128,128]{2,1,0:T(8,128)(2,1)S(1)}, bf16[16,128,128]{2,1,0:T(8,128)(2,1)S(1)}) custom-call(bf16[2,128,128,128]{3,2,1,0:T(8,128)(2,1)S(1)} %load.2.refs_0_, bf16[2,128,128,128]{3,2,1,0:T(8,128)(2,1)S(1)} %load.3.refs_1_, ...), custom_call_target="tpu_custom_call" | custom-call | flops 1073741824 | bytes 1048576 | tf_op jit(solution)/shard_map/pallas_call | solution.py:22
  35.3 4.2 %shard_map.48 = (bf16[16,128,128]{2,1,0:T(8,128)(2,1)S(1)}, bf16[16,128,128]{2,1,0:T(8,128)(2,1)S(1)}, bf16[16,128,128]{2,1,0:T(8,128)(2,1)S(1)}, bf16[16,128,128]{2,1,0:T(8,128)(2,1)S(1)}) custom-call(bf16[2,128,128,128]{3,2,1,0:T(8,128)(2,1)S(1)} %load.2.refs_0_, bf16[2,128,128,128]{3,2,1,0:T(8,128)(2,1)S(1)} %load.3.refs_1_, ...), custom_call_target="tpu_custom_call" | custom-call | flops 1073741824 | bytes 1048576 | tf_op jit(solution)/shard_map/pallas_call | solution.py:22
  42.5 4.0 %collective-permute-done.7.refs_3_ = bf16[16,128,128]{2,1,0:T(8,128)(2,1)S(1)} collective-permute-done((bf16[16,128,128]{2,1,0:T(8,128)(2,1)S(1)}, bf16[16,128,128]{2,1,0:T(8,128)(2,1)S(1)}, u32[]{:S(2)}, u32[]{:S(2)}) %collective-permute-start.7) | collective-permute-done | bytes 524320 | tf_op jit(solution)/shard_map/ppermute | solution.py:192
  46.5 2.5 %collective-permute-start.15 = (bf16[16,128,128]{2,1,0:T(8,128)(2,1)S(1)}, bf16[16,128,128]{2,1,0:T(8,128)(2,1)S(1)}, u32[]{:S(2)}, u32[]{:S(2)}) collective-permute-start(bf16[16,128,128]{2,1,0:T(8,128)(2,1)S(1)} %get-tuple-element.40), channel_id=1, source_target_pairs={{0,3},{1,2},{2,1},{3,0},{4,7},{5,6},{6,5},{7,4},{8,11},{9,10},{10,... | collective-permute-start | bytes 1572872 | tf_op jit(solution)/shard_map/ppermute | solution.py:192
  49.0 10.3 %collective-permute-done.8.refs_4_ = bf16[16,128,128]{2,1,0:T(8,128)(2,1)S(1)} collective-permute-done((bf16[16,128,128]{2,1,0:T(8,128)(2,1)S(1)}, bf16[16,128,128]{2,1,0:T(8,128)(2,1)S(1)}, u32[]{:S(2)}, u32[]{:S(2)}) %collective-permute-start.8) | collective-permute-done | bytes 524320 | tf_op jit(solution)/shard_map/ppermute | solution.py:192
  59.3 3.9 %collective-permute-start.23 = (bf16[16,128,128]{2,1,0:T(8,128)(2,1)S(1)}, bf16[16,128,128]{2,1,0:T(8,128)(2,1)S(1)}, u32[]{:S(2)}, u32[]{:S(2)}) collective-permute-start(bf16[16,128,128]{2,1,0:T(8,128)(2,1)S(1)} %get-tuple-element.37.refs_2_), channel_id=1, source_target_pairs={{0,28},{4,0},{8,4},{12,8},{16,12},{20,16},{24,20},{28,24},{1,29},{... | collective-permute-start | bytes 1572872 | tf_op jit(solution)/shard_map/ppermute | solution.py:189
  63.2 5.9 %collective-permute-done.13.refs_3_ = bf16[16,128,128]{2,1,0:T(8,128)(2,1)S(1)} collective-permute-done((bf16[16,128,128]{2,1,0:T(8,128)(2,1)S(1)}, bf16[16,128,128]{2,1,0:T(8,128)(2,1)S(1)}, u32[]{:S(2)}, u32[]{:S(2)}) %collective-permute-start.13) | collective-permute-done | bytes 524320 | tf_op jit(solution)/shard_map/ppermute | solution.py:192
  69.1 8.8 %collective-permute-done.14.refs_4_ = bf16[16,128,128]{2,1,0:T(8,128)(2,1)S(1)} collective-permute-done((bf16[16,128,128]{2,1,0:T(8,128)(2,1)S(1)}, bf16[16,128,128]{2,1,0:T(8,128)(2,1)S(1)}, u32[]{:S(2)}, u32[]{:S(2)}) %collective-permute-start.14) | collective-permute-done | bytes 524320 | tf_op jit(solution)/shard_map/ppermute | solution.py:192
  77.9 3.6 %collective-permute-start.25 = (bf16[16,128,128]{2,1,0:T(8,128)(2,1)S(1)}, bf16[16,128,128]{2,1,0:T(8,128)(2,1)S(1)}, u32[]{:S(2)}, u32[]{:S(2)}) collective-permute-start(bf16[16,128,128]{2,1,0:T(8,128)(2,1)S(1)} %collective-permute-done.14.refs_4_), channel_id=1, source_target_pairs={{0,28},{4,0},{8,4},{12,8},{16,12},{20,16},{24,20},{28,24},{1,29},{... | collective-permute-start | bytes 1572872 | tf_op jit(solution)/shard_map/ppermute | solution.py:189
  81.8 2.6 %shard_map.49 = (bf16[16,128,512]{2,1,0:T(8,128)(2,1)S(1)}, f32[128,128]{1,0:T(8,128)S(1)}) custom-call(s32[3]{0:T(128)S(1)} %pad_add_fusion.refs_0_, bf16[512,512]{1,0:T(8,128)(2,1)S(1)} %copy-done.3, bf16[16,128,128]{2,1,0:T(8,128)(2,1)S(1)} %get-tuple-element.37.refs_2_, bf16[16,128,128]{2,1,0:T(8,128)(2,1)S(1)} %collective-permute-done.13.refs_3_, ...), custom_call_target="tpu_custom_call" | custom-call | flops 1342177280 | bytes 1048576 | tf_op jit(solution)/shard_map/pallas_call | solution.py:22
  84.4 2.6 %shard_map.50 = (bf16[16,128,512]{2,1,0:T(8,128)(2,1)S(1)}, f32[128,128]{1,0:T(8,128)S(1)}) custom-call(s32[3]{0:T(128)S(1)} %pad_add_fusion.refs_0_, bf16[512,512]{1,0:T(8,128)(2,1)S(1)} %copy-done.3, bf16[16,128,128]{2,1,0:T(8,128)(2,1)S(1)} %get-tuple-element.29.refs_2_, bf16[16,128,128]{2,1,0:T(8,128)(2,1)S(1)} %collective-permute-done.7.refs_3_, ...), custom_call_target="tpu_custom_call" | custom-call | flops 1342177280 | bytes 1048576 | tf_op jit(solution)/shard_map/pallas_call | solution.py:22
  87.1 1.6 %collective-permute-start.17 = (f32[128,128]{1,0:T(8,128)S(1)}, f32[128,128]{1,0:T(8,128)S(1)}, u32[]{:S(2)}, u32[]{:S(2)}) collective-permute-start(f32[128,128]{1,0:T(8,128)S(1)} %get-tuple-element.42), channel_id=1, source_target_pairs={{0,2},{1,3},{2,0},{3,1},{4,6},{5,7},{6,4},{7,5},{8,10},{9,11},{10,... | collective-permute-start | bytes 196616 | tf_op jit(solution)/shard_map/ppermute | solution.py:192
  91.7 4.1 %collective-permute-done.26.refs_4_ = bf16[16,128,128]{2,1,0:T(8,128)(2,1)S(1)} collective-permute-done((bf16[16,128,128]{2,1,0:T(8,128)(2,1)S(1)}, bf16[16,128,128]{2,1,0:T(8,128)(2,1)S(1)}, u32[]{:S(2)}, u32[]{:S(2)}) %collective-permute-start.26) | collective-permute-done | bytes 524320 | tf_op jit(solution)/shard_map/ppermute | solution.py:189
  96.5 4.9 %collective-permute-done.21.refs_3_ = bf16[16,128,128]{2,1,0:T(8,128)(2,1)S(1)} collective-permute-done((bf16[16,128,128]{2,1,0:T(8,128)(2,1)S(1)}, bf16[16,128,128]{2,1,0:T(8,128)(2,1)S(1)}, u32[]{:S(2)}, u32[]{:S(2)}) %collective-permute-start.21) | collective-permute-done | bytes 524320 | tf_op jit(solution)/shard_map/ppermute | solution.py:189
  101.5 5.6 %collective-permute-done.22.refs_4_ = bf16[16,128,128]{2,1,0:T(8,128)(2,1)S(1)} collective-permute-done((bf16[16,128,128]{2,1,0:T(8,128)(2,1)S(1)}, bf16[16,128,128]{2,1,0:T(8,128)(2,1)S(1)}, u32[]{:S(2)}, u32[]{:S(2)}) %collective-permute-start.22) | collective-permute-done | bytes 524320 | tf_op jit(solution)/shard_map/ppermute | solution.py:189
  107.8 1.6 %collective-permute-start.28 = (f32[128,128]{1,0:T(8,128)S(1)}, f32[128,128]{1,0:T(8,128)S(1)}, u32[]{:S(2)}, u32[]{:S(2)}) collective-permute-start(f32[128,128]{1,0:T(8,128)S(1)} %shard_map.52), channel_id=1, source_target_pairs={{0,2},{1,3},{2,0},{3,1},{4,6},{5,7},{6,4},{7,5},{8,10},{9,11},{10,... | collective-permute-start | bytes 196616 | tf_op jit(solution)/shard_map/ppermute | solution.py:192
  109.4 1.9 %collective-permute-start.27 = (f32[128,128]{1,0:T(8,128)S(1)}, f32[128,128]{1,0:T(8,128)S(1)}, u32[]{:S(2)}, u32[]{:S(2)}) collective-permute-start(f32[128,128]{1,0:T(8,128)S(1)} %shard_map.52), channel_id=1, source_target_pairs={{0,1},{1,0},{2,3},{3,2},{4,5},{5,4},{6,7},{7,6},{8,9},{9,8},{10,11... | collective-permute-start | bytes 196616 | tf_op jit(solution)/shard_map/ppermute | solution.py:192
  112.1 2.4 %collective-permute-done.29 = f32[128,128]{1,0:T(8,128)S(1)} collective-permute-done((f32[128,128]{1,0:T(8,128)S(1)}, f32[128,128]{1,0:T(8,128)S(1)}, u32[]{:S(2)}, u32[]{:S(2)}) %collective-permute-start.29) | collective-permute-done | bytes 65568 | tf_op jit(solution)/shard_map/ppermute | solution.py:192
  (57 shorter events, 21.2 us)
Async XLA Ops:
  0.0 9.4 %collective-permute-start.3 = (bf16[4096,128]{1,0:T(8,128)(2,1)}, bf16[4096,128]{1,0:T(8,128)(2,1)S(1)}, u32[]{:S(2)}, u32[]{:S(2)}) collective-permute-start(bf16[4096,128]{1,0:T(8,128)(2,1)} %refs_5_.1), channel_id=1, source_target_pairs={{0,4},{4,0},{8,12},{12,8},{16,20},{20,16},{24,28},{28,24},{1,5},{5... | collective-permute-start | bytes 3145736 | tf_op jit(solution)/shard_map/ppermute | solution.py:197
  12.4 15.2 %collective-permute-start.4 = (bf16[4,64,128]{2,1,0:T(8,128)(2,1)S(1)}, bf16[4,64,128]{2,1,0:T(8,128)(2,1)S(1)}, u32[]{:S(2)}, u32[]{:S(2)}) collective-permute-start(bf16[4,64,128]{2,1,0:T(8,128)(2,1)S(1)} %get-tuple-element.26), channel_id=1, source_target_pairs={{0,24},{4,28},{8,0},{12,4},{16,8},{20,12},{24,16},{28,20},{1,25},{... | collective-permute-start | bytes 196616 | tf_op jit(solution)/shard_map/ppermute | solution.py:189
  15.6 12.0 %collective-permute-start.5 = (bf16[4,64,128]{2,1,0:T(8,128)(2,1)S(1)}, bf16[4,64,128]{2,1,0:T(8,128)(2,1)S(1)}, u32[]{:S(2)}, u32[]{:S(2)}) collective-permute-start(bf16[4,64,128]{2,1,0:T(8,128)(2,1)S(1)} %get-tuple-element.27), channel_id=1, source_target_pairs={{0,16},{4,20},{8,24},{12,28},{16,0},{20,4},{24,8},{28,12},{1,17},{... | collective-permute-start | bytes 196616 | tf_op jit(solution)/shard_map/ppermute | solution.py:189
  15.6 12.0 %collective-permute-start.6 = (bf16[4,64,128]{2,1,0:T(8,128)(2,1)S(1)}, bf16[4,64,128]{2,1,0:T(8,128)(2,1)S(1)}, u32[]{:S(2)}, u32[]{:S(2)}) collective-permute-start(bf16[4,64,128]{2,1,0:T(8,128)(2,1)S(1)} %get-tuple-element.28), channel_id=1, source_target_pairs={{0,8},{4,12},{8,16},{12,20},{16,24},{20,28},{24,0},{28,4},{1,9},{5... | collective-permute-start | bytes 196616 | tf_op jit(solution)/shard_map/ppermute | solution.py:189
  23.1 11.6 %collective-permute-start.10 = (bf16[4,64,128]{2,1,0:T(8,128)(2,1)S(1)}, bf16[4,64,128]{2,1,0:T(8,128)(2,1)S(1)}, u32[]{:S(2)}, u32[]{:S(2)}) collective-permute-start(bf16[4,64,128]{2,1,0:T(8,128)(2,1)S(1)} %get-tuple-element.34), channel_id=1, source_target_pairs={{0,24},{4,28},{8,0},{12,4},{16,8},{20,12},{24,16},{28,20},{1,25},{... | collective-permute-start | bytes 196616 | tf_op jit(solution)/shard_map/ppermute | solution.py:189
  26.4 8.9 %collective-permute-start.11 = (bf16[4,64,128]{2,1,0:T(8,128)(2,1)S(1)}, bf16[4,64,128]{2,1,0:T(8,128)(2,1)S(1)}, u32[]{:S(2)}, u32[]{:S(2)}) collective-permute-start(bf16[4,64,128]{2,1,0:T(8,128)(2,1)S(1)} %get-tuple-element.35), channel_id=1, source_target_pairs={{0,16},{4,20},{8,24},{12,28},{16,0},{20,4},{24,8},{28,12},{1,17},{... | collective-permute-start | bytes 196616 | tf_op jit(solution)/shard_map/ppermute | solution.py:189
  27.5 7.7 %collective-permute-start.12 = (bf16[4,64,128]{2,1,0:T(8,128)(2,1)S(1)}, bf16[4,64,128]{2,1,0:T(8,128)(2,1)S(1)}, u32[]{:S(2)}, u32[]{:S(2)}) collective-permute-start(bf16[4,64,128]{2,1,0:T(8,128)(2,1)S(1)} %get-tuple-element.36), channel_id=1, source_target_pairs={{0,8},{4,12},{8,16},{12,20},{16,24},{20,28},{24,0},{28,4},{1,9},{5... | collective-permute-start | bytes 196616 | tf_op jit(solution)/shard_map/ppermute | solution.py:189
  31.7 14.9 %collective-permute-start.7 = (bf16[16,128,128]{2,1,0:T(8,128)(2,1)S(1)}, bf16[16,128,128]{2,1,0:T(8,128)(2,1)S(1)}, u32[]{:S(2)}, u32[]{:S(2)}) collective-permute-start(bf16[16,128,128]{2,1,0:T(8,128)(2,1)S(1)} %get-tuple-element.30), channel_id=1, source_target_pairs={{0,1},{1,0},{2,3},{3,2},{4,5},{5,4},{6,7},{7,6},{8,9},{9,8},{10,11... | collective-permute-start | bytes 1572872 | tf_op jit(solution)/shard_map/ppermute | solution.py:192
  33.2 26.0 %collective-permute-start.8 = (bf16[16,128,128]{2,1,0:T(8,128)(2,1)S(1)}, bf16[16,128,128]{2,1,0:T(8,128)(2,1)S(1)}, u32[]{:S(2)}, u32[]{:S(2)}) collective-permute-start(bf16[16,128,128]{2,1,0:T(8,128)(2,1)S(1)} %get-tuple-element.31), channel_id=1, source_target_pairs={{0,2},{1,3},{2,0},{3,1},{4,6},{5,7},{6,4},{7,5},{8,10},{9,11},{10,... | collective-permute-start | bytes 1572872 | tf_op jit(solution)/shard_map/ppermute | solution.py:192
  34.8 24.5 %collective-permute-start.9 = (bf16[16,128,128]{2,1,0:T(8,128)(2,1)S(1)}, bf16[16,128,128]{2,1,0:T(8,128)(2,1)S(1)}, u32[]{:S(2)}, u32[]{:S(2)}) collective-permute-start(bf16[16,128,128]{2,1,0:T(8,128)(2,1)S(1)} %get-tuple-element.32), channel_id=1, source_target_pairs={{0,3},{1,2},{2,1},{3,0},{4,7},{5,6},{6,5},{7,4},{8,11},{9,10},{10,... | collective-permute-start | bytes 1572872 | tf_op jit(solution)/shard_map/ppermute | solution.py:192
  39.4 29.6 %collective-permute-start.13 = (bf16[16,128,128]{2,1,0:T(8,128)(2,1)S(1)}, bf16[16,128,128]{2,1,0:T(8,128)(2,1)S(1)}, u32[]{:S(2)}, u32[]{:S(2)}) collective-permute-start(bf16[16,128,128]{2,1,0:T(8,128)(2,1)S(1)} %get-tuple-element.38), channel_id=1, source_target_pairs={{0,1},{1,0},{2,3},{3,2},{4,5},{5,4},{6,7},{7,6},{8,9},{9,8},{10,11... | collective-permute-start | bytes 1572872 | tf_op jit(solution)/shard_map/ppermute | solution.py:192
  41.0 36.9 %collective-permute-start.14 = (bf16[16,128,128]{2,1,0:T(8,128)(2,1)S(1)}, bf16[16,128,128]{2,1,0:T(8,128)(2,1)S(1)}, u32[]{:S(2)}, u32[]{:S(2)}) collective-permute-start(bf16[16,128,128]{2,1,0:T(8,128)(2,1)S(1)} %get-tuple-element.39), channel_id=1, source_target_pairs={{0,2},{1,3},{2,0},{3,1},{4,6},{5,7},{6,4},{7,5},{8,10},{9,11},{10,... | collective-permute-start | bytes 1572872 | tf_op jit(solution)/shard_map/ppermute | solution.py:192
  46.5 31.4 %collective-permute-start.15 = (bf16[16,128,128]{2,1,0:T(8,128)(2,1)S(1)}, bf16[16,128,128]{2,1,0:T(8,128)(2,1)S(1)}, u32[]{:S(2)}, u32[]{:S(2)}) collective-permute-start(bf16[16,128,128]{2,1,0:T(8,128)(2,1)S(1)} %get-tuple-element.40), channel_id=1, source_target_pairs={{0,3},{1,2},{2,1},{3,0},{4,7},{5,6},{6,5},{7,4},{8,11},{9,10},{10,... | collective-permute-start | bytes 1572872 | tf_op jit(solution)/shard_map/ppermute | solution.py:192
  59.3 22.3 %collective-permute-start.19 = (bf16[16,128,128]{2,1,0:T(8,128)(2,1)S(1)}, bf16[16,128,128]{2,1,0:T(8,128)(2,1)S(1)}, u32[]{:S(2)}, u32[]{:S(2)}) collective-permute-start(bf16[16,128,128]{2,1,0:T(8,128)(2,1)S(1)} %get-tuple-element.29.refs_2_), channel_id=1, source_target_pairs={{0,28},{4,0},{8,4},{12,8},{16,12},{20,16},{24,20},{28,24},{1,29},{... | collective-permute-start | bytes 1572872 | tf_op jit(solution)/shard_map/ppermute | solution.py:189
  59.3 22.3 %collective-permute-start.23 = (bf16[16,128,128]{2,1,0:T(8,128)(2,1)S(1)}, bf16[16,128,128]{2,1,0:T(8,128)(2,1)S(1)}, u32[]{:S(2)}, u32[]{:S(2)}) collective-permute-start(bf16[16,128,128]{2,1,0:T(8,128)(2,1)S(1)} %get-tuple-element.37.refs_2_), channel_id=1, source_target_pairs={{0,28},{4,0},{8,4},{12,8},{16,12},{20,16},{24,20},{28,24},{1,29},{... | collective-permute-start | bytes 1572872 | tf_op jit(solution)/shard_map/ppermute | solution.py:189
  69.1 12.6 %collective-permute-start.20 = (bf16[16,128,128]{2,1,0:T(8,128)(2,1)S(1)}, bf16[16,128,128]{2,1,0:T(8,128)(2,1)S(1)}, u32[]{:S(2)}, u32[]{:S(2)}) collective-permute-start(bf16[16,128,128]{2,1,0:T(8,128)(2,1)S(1)} %collective-permute-done.7.refs_3_), channel_id=1, source_target_pairs={{0,28},{4,0},{8,4},{12,8},{16,12},{20,16},{24,20},{28,24},{1,29},{... | collective-permute-start | bytes 1572872 | tf_op jit(solution)/shard_map/ppermute | solution.py:189
  77.9 9.2 %collective-permute-start.24 = (bf16[16,128,128]{2,1,0:T(8,128)(2,1)S(1)}, bf16[16,128,128]{2,1,0:T(8,128)(2,1)S(1)}, u32[]{:S(2)}, u32[]{:S(2)}) collective-permute-start(bf16[16,128,128]{2,1,0:T(8,128)(2,1)S(1)} %collective-permute-done.13.refs_3_), channel_id=1, source_target_pairs={{0,28},{4,0},{8,4},{12,8},{16,12},{20,16},{24,20},{28,24},{1,29},{... | collective-permute-start | bytes 1572872 | tf_op jit(solution)/shard_map/ppermute | solution.py:189
  77.9 12.3 %collective-permute-start.25 = (bf16[16,128,128]{2,1,0:T(8,128)(2,1)S(1)}, bf16[16,128,128]{2,1,0:T(8,128)(2,1)S(1)}, u32[]{:S(2)}, u32[]{:S(2)}) collective-permute-start(bf16[16,128,128]{2,1,0:T(8,128)(2,1)S(1)} %collective-permute-done.14.refs_4_), channel_id=1, source_target_pairs={{0,28},{4,0},{8,4},{12,8},{16,12},{20,16},{24,20},{28,24},{1,29},{... | collective-permute-start | bytes 1572872 | tf_op jit(solution)/shard_map/ppermute | solution.py:189
  81.6 14.3 %collective-permute-start.26 = (bf16[16,128,128]{2,1,0:T(8,128)(2,1)S(1)}, bf16[16,128,128]{2,1,0:T(8,128)(2,1)S(1)}, u32[]{:S(2)}, u32[]{:S(2)}) collective-permute-start(bf16[16,128,128]{2,1,0:T(8,128)(2,1)S(1)} %collective-permute-done.15.refs_5_), channel_id=1, source_target_pairs={{0,28},{4,0},{8,4},{12,8},{16,12},{20,16},{24,20},{28,24},{1,29},{... | collective-permute-start | bytes 1572872 | tf_op jit(solution)/shard_map/ppermute | solution.py:189
  81.6 19.8 %collective-permute-start.21 = (bf16[16,128,128]{2,1,0:T(8,128)(2,1)S(1)}, bf16[16,128,128]{2,1,0:T(8,128)(2,1)S(1)}, u32[]{:S(2)}, u32[]{:S(2)}) collective-permute-start(bf16[16,128,128]{2,1,0:T(8,128)(2,1)S(1)} %collective-permute-done.8.refs_4_), channel_id=1, source_target_pairs={{0,28},{4,0},{8,4},{12,8},{16,12},{20,16},{24,20},{28,24},{1,29},{... | collective-permute-start | bytes 1572872 | tf_op jit(solution)/shard_map/ppermute | solution.py:189
  81.7 25.4 %collective-permute-start.22 = (bf16[16,128,128]{2,1,0:T(8,128)(2,1)S(1)}, bf16[16,128,128]{2,1,0:T(8,128)(2,1)S(1)}, u32[]{:S(2)}, u32[]{:S(2)}) collective-permute-start(bf16[16,128,128]{2,1,0:T(8,128)(2,1)S(1)} %collective-permute-done.9.refs_5_), channel_id=1, source_target_pairs={{0,28},{4,0},{8,4},{12,8},{16,12},{20,16},{24,20},{28,24},{1,29},{... | collective-permute-start | bytes 1572872 | tf_op jit(solution)/shard_map/ppermute | solution.py:189
  87.1 22.3 %collective-permute-start.17 = (f32[128,128]{1,0:T(8,128)S(1)}, f32[128,128]{1,0:T(8,128)S(1)}, u32[]{:S(2)}, u32[]{:S(2)}) collective-permute-start(f32[128,128]{1,0:T(8,128)S(1)} %get-tuple-element.42), channel_id=1, source_target_pairs={{0,2},{1,3},{2,0},{3,1},{4,6},{5,7},{6,4},{7,5},{8,10},{9,11},{10,... | collective-permute-start | bytes 196616 | tf_op jit(solution)/shard_map/ppermute | solution.py:192
  90.2 21.1 %collective-permute-start.18 = (f32[128,128]{1,0:T(8,128)S(1)}, f32[128,128]{1,0:T(8,128)S(1)}, u32[]{:S(2)}, u32[]{:S(2)}) collective-permute-start(f32[128,128]{1,0:T(8,128)S(1)} %get-tuple-element.42), channel_id=1, source_target_pairs={{0,3},{1,2},{2,1},{3,0},{4,7},{5,6},{6,5},{7,4},{8,11},{9,10},{10,... | collective-permute-start | bytes 196616 | tf_op jit(solution)/shard_map/ppermute | solution.py:192
  95.8 15.5 %collective-permute-start.16 = (f32[128,128]{1,0:T(8,128)S(1)}, f32[128,128]{1,0:T(8,128)S(1)}, u32[]{:S(2)}, u32[]{:S(2)}) collective-permute-start(f32[128,128]{1,0:T(8,128)S(1)} %get-tuple-element.42), channel_id=1, source_target_pairs={{0,1},{1,0},{2,3},{3,2},{4,5},{5,4},{6,7},{7,6},{8,9},{9,8},{10,11... | collective-permute-start | bytes 196616 | tf_op jit(solution)/shard_map/ppermute | solution.py:192
  (10 other events, 83.9 us)

commit v2 on v1

v2 whole, which is shorter than its diff:
```python
import functools

import jax
import jax.numpy as jnp
from jax import lax
from jax.experimental import pallas as pl
from jax.experimental.pallas import tpu as pltpu
from jax.sharding import PartitionSpec as P


PARTS = (1, 1)
PIECES = (2, 2)
STEP_ROWS = 16
GROUP = 4
LONG = 20_000_000_000
VMEM = pltpu.VMEM
SMEM_SPEC = pl.BlockSpec(memory_space=pltpu.SMEM)
VMEM_SPEC = pl.BlockSpec(memory_space=pltpu.VMEM)


def local_call(kernel, out_shape, operands, scalars, flops, scratch=()):
    operands = [pltpu.with_memory_space_constraint(x, VMEM) for x in operands]
    out_shape = jax.tree.map(lambda x: VMEM(x.shape, x.dtype), out_shape)
    return pl.pallas_call(
        kernel,
        out_shape=out_shape,
        in_specs=[SMEM_SPEC] * len(scalars) + [VMEM_SPEC] * len(operands),
        out_specs=jax.tree.map(lambda _: VMEM_SPEC, out_shape),
        scratch_shapes=list(scratch),
        cost_estimate=pl.CostEstimate(flops=flops, bytes_accessed=1 << 20, transcendentals=0),
        compiler_params=pltpu.CompilerParams(vmem_limit_bytes=12 << 20),
    )(*scalars, *operands)


def turn_kernel(aux_count, place_ref, metric_ref, turned_ref):
    width = metric_ref.shape[0] // aux_count
    me = place_ref[2]
    for row in range(aux_count):
        for column in range(aux_count):
            turned_ref[row * width : (row + 1) * width, column * width : (column + 1) * width] = (
                metric_ref[
                    pl.ds(pl.multiple_of((me ^ row) * width, width), width),
                    pl.ds(pl.multiple_of((me ^ column) * width, width), width),
                ]
            )


def pick_kernel(owned, block, slot_count, aux_count, chunk_rows, *refs):
    dest_count = (len(refs) - 4) // (1 + len(chunk_rows))
    place_ref = refs[0]
    wanted = refs[1 : 1 + dest_count]
    own_ref, partner_ref = refs[1 + dest_count : 3 + dest_count]
    given = refs[3 + dest_count : -1]
    turned = refs[-1]
    base, core, me = place_ref[0], place_ref[1], place_ref[2]
    share = turned.shape[0] // aux_count
    for dest in range(dest_count):
        for slot in range(slot_count):
            orbital = wanted[dest][slot, 1]
            local = orbital - base
            inside = (orbital >= 0) & (local >= 0) & (local < 2 * owned)
            upper = jnp.where(local >= owned, 1, 0)
            row = jnp.clip(local - upper * owned, 0, owned - 1) * block
            rows = pl.ds(pl.multiple_of(row, block), block)
            picked = jnp.where(
                upper == core, own_ref[rows, :].astype(jnp.float32), partner_ref[rows, :].astype(jnp.float32)
            )
            picked = jnp.where(inside, picked, jnp.zeros_like(picked))
            turned[...] = picked.T
            for away in range(aux_count):
                start = pl.multiple_of((me ^ away) * share, share)
                first = 0
                for chunk, count in enumerate(chunk_rows):
                    given[dest * len(chunk_rows) + chunk][slot, away * count : (away + 1) * count, :] = turned[
                        pl.ds(start + first, count), :
                    ].astype(jnp.bfloat16)
                    first += count


def half_kernel(out_count, *refs):
    tile_ref = refs[0]
    parts = refs[1 : -1 - out_count]
    outs = refs[-1 - out_count : -1]
    wide = refs[-1]
    slot_count, block = tile_ref.shape[:2]
    width = parts[0].shape[1]
    rows = STEP_ROWS
    stride = rows + 1
    columns = []
    for slot in range(slot_count):
        total = parts[0][slot].astype(jnp.float32)
        for part in parts[1:]:
            total = total + part[slot].astype(jnp.float32)
        columns.append(total.astype(jnp.bfloat16))
    left = jnp.concatenate(columns, axis=1)

    def step(index, carry):
        base = pl.multiple_of(index * rows, rows)
        for row in range(0, rows, 2):
            right = jnp.concatenate(
                [
                    tile_ref[:, base + row + m].reshape(slot_count * block, block) for m in range(2)
                ],
                axis=1,
            )
            product = jnp.dot(left, right, preferred_element_type=jnp.float32)
            wide[pl.ds(row, width, stride=stride), :] = product[:, :block]
            wide[pl.ds(row + 1, width, stride=stride), :] = product[:, block:]
        first = 0
        for out in outs:
            for i in range(out.shape[0]):
                out[i, pl.ds(base, rows), :] = wide[pl.ds((first + i) * stride, rows), :].astype(
                    jnp.bfloat16
                )
            first += out.shape[0]
        return carry

    lax.fori_loop(0, block // rows, step, 0)


def gram(fitted, parts, first):
    count = len(fitted)
    right = [
        part[i if part is parts[-1] else first + i] for i in range(count) for part in parts
    ]
    return lax.dot_general(
        jnp.concatenate(fitted, axis=1),
        jnp.concatenate(right, axis=1),
        (((1,), (1,)), ((), ())),
        preferred_element_type=jnp.float32,
    )


def fit_kernel(aux_count, first, *refs):
    metric_ref = refs[0]
    parts = refs[1 : 1 + aux_count]
    before = refs[1 + aux_count : -2]
    fitted_ref, after_ref = refs[-2:]
    count, block, width = parts[-1].shape
    metric = metric_ref[...]
    for start in range(0, count, GROUP):
        here = min(GROUP, count - start)
        rows = [part[first + start : first + start + here] for part in parts[:-1]]
        rows.append(parts[-1][start : start + here])
        half = jnp.concatenate([x.reshape(here * block, width) for x in rows], axis=1)
        fitted = jnp.dot(half, metric, preferred_element_type=jnp.float32).astype(jnp.bfloat16)
        fitted_ref[start : start + here] = fitted.reshape(here, block, aux_count * width)
    total = gram([fitted_ref[i] for i in range(count)], parts, first)
    for ref in before:
        total = total + ref[...]
    after_ref[...] = total


def couple_kernel(aux_count, first, final, *refs):
    total = gram([refs[0][i] for i in range(refs[0].shape[0])], refs[1 : 1 + aux_count], first)
    before = refs[1 + aux_count : -1]
    if final:
        before, diagonal = before[:-1], before[-1]
    for ref in before:
        total = total + ref[...]
    if final:
        block = total.shape[0]
        refs[-1][:, :block] = diagonal[...].astype(jnp.bfloat16)
        refs[-1][:, block:] = total.astype(jnp.bfloat16)
    else:
        refs[-1][...] = total


def on_device(orb_count, aux_count, three_center, screening, density_factor, metric_inverse):
    slot_count, block = three_center.shape[:2]
    occupied = density_factor.shape[1]
    owned = density_factor.shape[0] // block
    share = occupied // aux_count
    chunk_rows = [share * part // sum(PARTS) for part in PARTS]
    chunks = len(chunk_rows)
    bf16, f32 = jnp.bfloat16, jnp.float32

    orb = lax.axis_index("orb")
    aux = lax.axis_index("aux")
    place = jnp.stack([(orb >> 1) * (2 * owned), orb & 1, aux]).astype(jnp.int32)

    def along_orb(x, by):
        return lax.ppermute(x, "orb", [(i, (i + by) % orb_count) for i in range(orb_count)])

    def same_core(x, chip):
        return lax.ppermute(x, "orb", [(i, i ^ (2 * chip)) for i in range(orb_count)])

    def across_aux(x, away):
        return lax.ppermute(x, "aux", [(i, i ^ away) for i in range(aux_count)])

    turned = local_call(
        functools.partial(turn_kernel, aux_count),
        jax.ShapeDtypeStruct(metric_inverse.shape, bf16),
        [metric_inverse],
        [place],
        LONG,
    )
    partner = lax.ppermute(density_factor, "orb", [(i, i ^ 1) for i in range(orb_count)])
    wanted = [screening]
    chips = range(1, orb_count // 2)
    for chip in chips:
        wanted.append(same_core(screening, chip))
    given = local_call(
        functools.partial(pick_kernel, owned, block, slot_count, aux_count, chunk_rows),
        [
            jax.ShapeDtypeStruct((slot_count, aux_count * count, block), bf16)
            for _ in wanted
            for count in chunk_rows
        ],
        [density_factor, partner],
        [place, *wanted],
        LONG,
        [pltpu.VMEM((occupied, block), f32)],
    )
    last = aux_count - 1
    pieces = []
    for c, count in enumerate(chunk_rows):
        arrived = [given[c]]
        for chip in chips:
            arrived.append(same_core(given[chip * chunks + c], chip))
        piece_rows = count // PIECES[c]
        out_rows = [count] * last + [piece_rows] * PIECES[c]
        halves = local_call(
            functools.partial(half_kernel, len(out_rows)),
            [jax.ShapeDtypeStruct((rows, block, block), bf16) for rows in out_rows],
            [three_center, *arrived],
            [],
            2 * slot_count * block**3 * count * aux_count,
            [pltpu.VMEM((aux_count * count * (STEP_ROWS + 1), block), f32)],
        )
        mine, theirs = [halves[0]], []
        for away in range(1, last):
            mine.append(across_aux(halves[away], away))
        for away in range(last):
            theirs.append(along_orb(mine[away], -1))
        for j in range(PIECES[c]):
            mine_piece = across_aux(halves[last + j], last)
            their_piece = along_orb(mine_piece, -1)
            pieces.append((c, j, piece_rows, mine + [mine_piece], theirs + [their_piece]))

    diagonal, coupling = [], []
    width = aux_count * block
    for number, (c, j, count, mine, theirs) in enumerate(pieces):
        final = number == len(pieces) - 1
        fitted, *diagonal = local_call(
            functools.partial(fit_kernel, aux_count, j * count),
            [
                jax.ShapeDtypeStruct((count, block, width), bf16),
                jax.ShapeDtypeStruct((block, block), f32),
            ],
            [turned, *mine, *diagonal],
            [],
            2 * count * block * width * (width + block),
        )
        coupling = [
            local_call(
                functools.partial(couple_kernel, aux_count, j * count, final),
                jax.ShapeDtypeStruct((block, 2 * block), bf16)
                if final
                else jax.ShapeDtypeStruct((block, block), f32),
                [fitted, *theirs, *coupling, *(diagonal if final else [])],
                [],
                2 * count * block * width * block,
            )
        ]

    terms = {0: coupling[0]}
    for away in reversed(range(1, aux_count)):
        terms[away] = across_aux(coupling[0], away)
    terms = [terms[away].astype(f32) for away in range(aux_count)]
    while len(terms) > 1:
        terms = [a + b for a, b in zip(terms[::2], terms[1::2])]
    return terms[0].astype(bf16)


def solution(mesh):
    placed = (P(("orb", "aux"), None, None, None), P(("orb", "aux"), None), P("orb", None), P())
    sizes = mesh.shape["orb"], mesh.shape["aux"]

    def body(*args):
        return on_device(*sizes, *args)

    return jax.shard_map(body, mesh=mesh, in_specs=placed, out_specs=P("orb", None), check_vma=False)
```

time: 116 us -> 116 us (level)
  starting transfers between devices: 38.7 us -> 46 us
  local copies, waits for them, and re-layouts: 7.68 us -> 1.93 us
    ppermute x0 -> x9, starting transfers between devices: none -> 14 us  [same_core(): return lax.ppermute(x, 'orb', [(i, i ^ 2 * chip) for i in range(orb_count)])]
    ppermute x0 -> x9, waiting for transfers between devices: none -> 10.6 us  [same_core(): return lax.ppermute(x, 'orb', [(i, i ^ 2 * chip) for i in range(orb_count)])]
    ppermute x12 -> x11, waiting for transfers between devices: 32.2 us -> 22.4 us  [across_aux(): return lax.ppermute(x, 'aux', [(i, i ^ away) for i in range(aux_count)])]
    ppermute x17 -> x10, starting transfers between devices: 22.5 us -> 16.5 us  [along_orb(): lax.ppermute(x, 'orb', [(i, (i + by) % orb_count) for i in range(orb_coun...]
    unnamed x8 -> x14, local copies, waits for them, and re-layouts: 7.68 us -> 1.93 us
    ppermute x17 -> x10, waiting for transfers between devices: 18.6 us -> 17.1 us  [along_orb(): lax.ppermute(x, 'orb', [(i, (i + by) % orb_count) for i in range(orb_coun...]
    ppermute x12 -> x11, starting transfers between devices: 15.8 us -> 15 us  [across_aux(): return lax.ppermute(x, 'aux', [(i, i ^ away) for i in range(aux_count)])]
    pallas_call x7 -> x12, Pallas kernels: 16 us -> 16.5 us  [local_call(): pl.pallas_call(kernel, out_shape=out_shape, in_specs=[SMEM_SPEC] * len(sc...]
  transfers between devices with their start and end apart: 30 -> 31, of which waited for: 12 -> 17; matrix products, arithmetic and copies ran while one was open for 0% -> 0% of each run, Pallas kernels for 14% -> 9%
where the time goes in v2:
time: 116 us; the launch traced here: 115 us
  waiting for transfers between devices  50 us (43%)
  starting transfers between devices  46 us (40%)
  Pallas kernels  16.5 us (14%)
  local copies, waits for them, and re-layouts  1.93 us (2%)
    ppermute x11, waiting for transfers between devices, across_aux(): return lax.ppermute(x, 'aux', [(i, i ^ away) for i in range(aux_count)])  22.4 us
    ppermute x10, waiting for transfers between devices, along_orb(): lax.ppermute(x, 'orb', [(i, (i + by) % orb_count) for i in range(orb_coun...  17.1 us
    ppermute x10, starting transfers between devices, along_orb(): lax.ppermute(x, 'orb', [(i, (i + by) % orb_count) for i in range(orb_coun...  16.5 us
    pallas_call x12, Pallas kernels, local_call(): pl.pallas_call(kernel, out_shape=out_shape, in_specs=[SMEM_SPEC] * len(sc...  16.5 us
    ppermute x11, starting transfers between devices, across_aux(): return lax.ppermute(x, 'aux', [(i, i ^ away) for i in range(aux_count)])  15 us
    ppermute x9, starting transfers between devices, same_core(): return lax.ppermute(x, 'orb', [(i, i ^ 2 * chip) for i in range(orb_count)])  14 us
    ppermute x9, waiting for transfers between devices, same_core(): return lax.ppermute(x, 'orb', [(i, i ^ 2 * chip) for i in range(orb_count)])  10.6 us
  transfers between devices with their start and end apart: 31, of which 17 were waited for; matrix products, arithmetic and copies ran while one was open for 0% of the time, Pallas kernels for 9%

profile of v2, /device:TPU:0, one launch (start us, length us, event | category | flops | bytes accessed | tf_op | source)
XLA Modules:
  0.0 115.3 jit_solution(15563832979383070907)
XLA Ops:
  0.5 2.6 %collective-permute-start = (s32[4,3]{1,0:T(4,128)}, s32[4,3]{1,0:T(4,128)S(1)}, u32[]{:S(2)}, u32[]{:S(2)}) collective-permute-start(s32[4,3]{1,0:T(4,128)} %refs_1_.1), channel_id=1, source_target_pairs={{0,8},{4,12},{8,0},{12,4},{16,24},{20,28},{24,16},{28,20},{1,9},{5... | collective-permute-start | bytes 152 | tf_op jit(solution)/shard_map/ppermute | solution.py:186
  3.1 2.6 %collective-permute-start.1 = (s32[4,3]{1,0:T(4,128)}, s32[4,3]{1,0:T(4,128)S(1)}, u32[]{:S(2)}, u32[]{:S(2)}) collective-permute-start(s32[4,3]{1,0:T(4,128)} %refs_1_.1), channel_id=1, source_target_pairs={{0,16},{4,20},{8,24},{12,28},{16,0},{20,4},{24,8},{28,12},{1,17},{... | collective-permute-start | bytes 152 | tf_op jit(solution)/shard_map/ppermute | solution.py:186
  5.7 2.0 %collective-permute-done.1.refs_3_ = s32[4,3]{1,0:T(4,128)S(1)} collective-permute-done((s32[4,3]{1,0:T(4,128)}, s32[4,3]{1,0:T(4,128)S(1)}, u32[]{:S(2)}, u32[]{:S(2)}) %collective-permute-start.1) | collective-permute-done | bytes 80 | tf_op jit(solution)/shard_map/ppermute | solution.py:186
  7.8 3.5 %collective-permute-done.2.refs_4_ = s32[4,3]{1,0:T(4,128)S(1)} collective-permute-done((s32[4,3]{1,0:T(4,128)}, s32[4,3]{1,0:T(4,128)S(1)}, u32[]{:S(2)}, u32[]{:S(2)}) %collective-permute-start.2) | collective-permute-done | bytes 80 | tf_op jit(solution)/shard_map/ppermute | solution.py:186
  14.2 2.1 %collective-permute-start.12 = (bf16[4,64,128]{2,1,0:T(8,128)(2,1)S(1)}, bf16[4,64,128]{2,1,0:T(8,128)(2,1)S(1)}, u32[]{:S(2)}, u32[]{:S(2)}) collective-permute-start(bf16[4,64,128]{2,1,0:T(8,128)(2,1)S(1)} %get-tuple-element.42), channel_id=1, source_target_pairs={{0,16},{4,20},{8,24},{12,28},{16,0},{20,4},{24,8},{28,12},{1,17},{... | collective-permute-start | bytes 196616 | tf_op jit(solution)/shard_map/ppermute | solution.py:186
  16.4 2.2 %collective-permute-start.13 = (bf16[4,64,128]{2,1,0:T(8,128)(2,1)S(1)}, bf16[4,64,128]{2,1,0:T(8,128)(2,1)S(1)}, u32[]{:S(2)}, u32[]{:S(2)}) collective-permute-start(bf16[4,64,128]{2,1,0:T(8,128)(2,1)S(1)} %get-tuple-element.43), channel_id=1, source_target_pairs={{0,24},{4,28},{8,16},{12,20},{16,8},{20,12},{24,0},{28,4},{1,25},{... | collective-permute-start | bytes 196616 | tf_op jit(solution)/shard_map/ppermute | solution.py:186
  18.6 2.6 %collective-permute-done.12.refs_3_ = bf16[4,64,128]{2,1,0:T(8,128)(2,1)S(1)} collective-permute-done((bf16[4,64,128]{2,1,0:T(8,128)(2,1)S(1)}, bf16[4,64,128]{2,1,0:T(8,128)(2,1)S(1)}, u32[]{:S(2)}, u32[]{:S(2)}) %collective-permute-start.12) | collective-permute-done | bytes 65568 | tf_op jit(solution)/shard_map/ppermute | solution.py:186
  22.6 4.1 %shard_map.49 = (bf16[16,128,128]{2,1,0:T(8,128)(2,1)S(1)}, bf16[16,128,128]{2,1,0:T(8,128)(2,1)S(1)}, bf16[16,128,128]{2,1,0:T(8,128)(2,1)S(1)}, bf16[8,128,128...) custom-call(bf16[4,128,128,128]{3,2,1,0:T(8,128)(2,1)S(1)} %bitcast.4, bf16[4,64,128]{2,1,0:T(8,128)(2,1)S(1)} %get-tuple-element.40.refs_1_, ...), custom_call_target="tpu_custom_call" | custom-call | flops 1073741824 | bytes 1048576 | tf_op jit(solution)/shard_map/pallas_call | solution.py:24
  26.7 2.6 %collective-permute-start.17 = (bf16[8,128,128]{2,1,0:T(8,128)(2,1)S(1)}, bf16[8,128,128]{2,1,0:T(8,128)(2,1)S(1)}, u32[]{:S(2)}, u32[]{:S(2)}) collective-permute-start(bf16[8,128,128]{2,1,0:T(8,128)(2,1)S(1)} %get-tuple-element.48), channel_id=1, source_target_pairs={{0,3},{1,2},{2,1},{3,0},{4,7},{5,6},{6,5},{7,4},{8,11},{9,10},{10,... | collective-permute-start | bytes 786440 | tf_op jit(solution)/shard_map/ppermute | solution.py:189
  29.3 2.6 %collective-permute-start.5 = (bf16[4,64,128]{2,1,0:T(8,128)(2,1)S(1)}, bf16[4,64,128]{2,1,0:T(8,128)(2,1)S(1)}, u32[]{:S(2)}, u32[]{:S(2)}) collective-permute-start(bf16[4,64,128]{2,1,0:T(8,128)(2,1)S(1)} %get-tuple-element.33), channel_id=1, source_target_pairs={{0,16},{4,20},{8,24},{12,28},{16,0},{20,4},{24,8},{28,12},{1,17},{... | collective-permute-start | bytes 196616 | tf_op jit(solution)/shard_map/ppermute | solution.py:186
  35.0 2.2 %collective-permute-start.16 = (bf16[8,128,128]{2,1,0:T(8,128)(2,1)S(1)}, bf16[8,128,128]{2,1,0:T(8,128)(2,1)S(1)}, u32[]{:S(2)}, u32[]{:S(2)}) collective-permute-start(bf16[8,128,128]{2,1,0:T(8,128)(2,1)S(1)} %get-tuple-element.47), channel_id=1, source_target_pairs={{0,3},{1,2},{2,1},{3,0},{4,7},{5,6},{6,5},{7,4},{8,11},{9,10},{10,... | collective-permute-start | bytes 786440 | tf_op jit(solution)/shard_map/ppermute | solution.py:189
  38.0 4.2 %shard_map.48 = (bf16[16,128,128]{2,1,0:T(8,128)(2,1)S(1)}, bf16[16,128,128]{2,1,0:T(8,128)(2,1)S(1)}, bf16[16,128,128]{2,1,0:T(8,128)(2,1)S(1)}, bf16[8,128,128...) custom-call(bf16[4,128,128,128]{3,2,1,0:T(8,128)(2,1)S(1)} %bitcast.4, bf16[4,64,128]{2,1,0:T(8,128)(2,1)S(1)} %get-tuple-element.31.refs_1_, ...), custom_call_target="tpu_custom_call" | custom-call | flops 1073741824 | bytes 1048576 | tf_op jit(solution)/shard_map/pallas_call | solution.py:24
  42.7 2.5 %collective-permute-start.9 = (bf16[8,128,128]{2,1,0:T(8,128)(2,1)S(1)}, bf16[8,128,128]{2,1,0:T(8,128)(2,1)S(1)}, u32[]{:S(2)}, u32[]{:S(2)}) collective-permute-start(bf16[8,128,128]{2,1,0:T(8,128)(2,1)S(1)} %get-tuple-element.38), channel_id=1, source_target_pairs={{0,3},{1,2},{2,1},{3,0},{4,7},{5,6},{6,5},{7,4},{8,11},{9,10},{10,... | collective-permute-start | bytes 786440 | tf_op jit(solution)/shard_map/ppermute | solution.py:189
  45.2 9.0 %collective-permute-done.16.refs_4_ = bf16[8,128,128]{2,1,0:T(8,128)(2,1)S(1)} collective-permute-done((bf16[8,128,128]{2,1,0:T(8,128)(2,1)S(1)}, bf16[8,128,128]{2,1,0:T(8,128)(2,1)S(1)}, u32[]{:S(2)}, u32[]{:S(2)}) %collective-permute-start.16) | collective-permute-done | bytes 262176 | tf_op jit(solution)/shard_map/ppermute | solution.py:189
  54.2 5.6 %collective-permute-done.10.refs_4_ = bf16[8,128,128]{2,1,0:T(8,128)(2,1)S(1)} collective-permute-done((bf16[8,128,128]{2,1,0:T(8,128)(2,1)S(1)}, bf16[8,128,128]{2,1,0:T(8,128)(2,1)S(1)}, u32[]{:S(2)}, u32[]{:S(2)}) %collective-permute-start.10) | collective-permute-done | bytes 262176 | tf_op jit(solution)/shard_map/ppermute | solution.py:189
  61.0 4.4 %collective-permute-done.9.refs_4_ = bf16[8,128,128]{2,1,0:T(8,128)(2,1)S(1)} collective-permute-done((bf16[8,128,128]{2,1,0:T(8,128)(2,1)S(1)}, bf16[8,128,128]{2,1,0:T(8,128)(2,1)S(1)}, u32[]{:S(2)}, u32[]{:S(2)}) %collective-permute-start.9) | collective-permute-done | bytes 262176 | tf_op jit(solution)/shard_map/ppermute | solution.py:189
  66.9 2.2 %collective-permute-start.26 = (bf16[8,128,128]{2,1,0:T(8,128)(2,1)S(1)}, bf16[8,128,128]{2,1,0:T(8,128)(2,1)S(1)}, u32[]{:S(2)}, u32[]{:S(2)}) collective-permute-start(bf16[8,128,128]{2,1,0:T(8,128)(2,1)S(1)} %collective-permute-done.16.refs_4_), channel_id=1, source_target_pairs={{0,28},{4,0},{8,4},{12,8},{16,12},{20,16},{24,20},{28,24},{1,29},{... | collective-permute-start | bytes 786440 | tf_op jit(solution)/shard_map/ppermute | solution.py:183
  70.7 3.7 %collective-permute-start.24 = (bf16[16,128,128]{2,1,0:T(8,128)(2,1)S(1)}, bf16[16,128,128]{2,1,0:T(8,128)(2,1)S(1)}, u32[]{:S(2)}, u32[]{:S(2)}) collective-permute-start(bf16[16,128,128]{2,1,0:T(8,128)(2,1)S(1)} %collective-permute-done.14.refs_2_), channel_id=1, source_target_pairs={{0,28},{4,0},{8,4},{12,8},{16,12},{20,16},{24,20},{28,24},{1,29},{... | collective-permute-start | bytes 1572872 | tf_op jit(solution)/shard_map/ppermute | solution.py:183
  74.4 2.8 %collective-permute-start.25 = (bf16[16,128,128]{2,1,0:T(8,128)(2,1)S(1)}, bf16[16,128,128]{2,1,0:T(8,128)(2,1)S(1)}, u32[]{:S(2)}, u32[]{:S(2)}) collective-permute-start(bf16[16,128,128]{2,1,0:T(8,128)(2,1)S(1)} %collective-permute-done.15.refs_3_), channel_id=1, source_target_pairs={{0,28},{4,0},{8,4},{12,8},{16,12},{20,16},{24,20},{28,24},{1,29},{... | collective-permute-start | bytes 1572872 | tf_op jit(solution)/shard_map/ppermute | solution.py:183
  78.3 6.5 %collective-permute-done.24.refs_2_ = bf16[16,128,128]{2,1,0:T(8,128)(2,1)S(1)} collective-permute-done((bf16[16,128,128]{2,1,0:T(8,128)(2,1)S(1)}, bf16[16,128,128]{2,1,0:T(8,128)(2,1)S(1)}, u32[]{:S(2)}, u32[]{:S(2)}) %collective-permute-start.24) | collective-permute-done | bytes 524320 | tf_op jit(solution)/shard_map/ppermute | solution.py:183
  84.8 3.7 %collective-permute-start.22 = (bf16[8,128,128]{2,1,0:T(8,128)(2,1)S(1)}, bf16[8,128,128]{2,1,0:T(8,128)(2,1)S(1)}, u32[]{:S(2)}, u32[]{:S(2)}) collective-permute-start(bf16[8,128,128]{2,1,0:T(8,128)(2,1)S(1)} %collective-permute-done.10.refs_4_), channel_id=1, source_target_pairs={{0,28},{4,0},{8,4},{12,8},{16,12},{20,16},{24,20},{28,24},{1,29},{... | collective-permute-start | bytes 786440 | tf_op jit(solution)/shard_map/ppermute | solution.py:183
  90.4 3.7 %collective-permute-start.21 = (bf16[8,128,128]{2,1,0:T(8,128)(2,1)S(1)}, bf16[8,128,128]{2,1,0:T(8,128)(2,1)S(1)}, u32[]{:S(2)}, u32[]{:S(2)}) collective-permute-start(bf16[8,128,128]{2,1,0:T(8,128)(2,1)S(1)} %collective-permute-done.9.refs_4_), channel_id=1, source_target_pairs={{0,28},{4,0},{8,4},{12,8},{16,12},{20,16},{24,20},{28,24},{1,29},{... | collective-permute-start | bytes 786440 | tf_op jit(solution)/shard_map/ppermute | solution.py:183
  99.8 4.6 %collective-permute-done.22.refs_4_ = bf16[8,128,128]{2,1,0:T(8,128)(2,1)S(1)} collective-permute-done((bf16[8,128,128]{2,1,0:T(8,128)(2,1)S(1)}, bf16[8,128,128]{2,1,0:T(8,128)(2,1)S(1)}, u32[]{:S(2)}, u32[]{:S(2)}) %collective-permute-start.22) | collective-permute-done | bytes 262176 | tf_op jit(solution)/shard_map/ppermute | solution.py:183
  104.9 2.4 %collective-permute-done.21.refs_4_ = bf16[8,128,128]{2,1,0:T(8,128)(2,1)S(1)} collective-permute-done((bf16[8,128,128]{2,1,0:T(8,128)(2,1)S(1)}, bf16[8,128,128]{2,1,0:T(8,128)(2,1)S(1)}, u32[]{:S(2)}, u32[]{:S(2)}) %collective-permute-start.21) | collective-permute-done | bytes 262176 | tf_op jit(solution)/shard_map/ppermute | solution.py:183
  (67 shorter events, 30.9 us)
Async XLA Ops:
  0.0 11.2 %collective-permute-start.3 = (bf16[4096,128]{1,0:T(8,128)(2,1)}, bf16[4096,128]{1,0:T(8,128)(2,1)S(1)}, u32[]{:S(2)}, u32[]{:S(2)}) collective-permute-start(bf16[4096,128]{1,0:T(8,128)(2,1)} %refs_5_.1), channel_id=1, source_target_pairs={{0,4},{4,0},{8,12},{12,8},{16,20},{20,16},{24,28},{28,24},{1,5},{5... | collective-permute-start | bytes 3145736 | tf_op jit(solution)/shard_map/ppermute | solution.py:198
  0.5 5.2 %collective-permute-start = (s32[4,3]{1,0:T(4,128)}, s32[4,3]{1,0:T(4,128)S(1)}, u32[]{:S(2)}, u32[]{:S(2)}) collective-permute-start(s32[4,3]{1,0:T(4,128)} %refs_1_.1), channel_id=1, source_target_pairs={{0,8},{4,12},{8,0},{12,4},{16,24},{20,28},{24,16},{28,20},{1,9},{5... | collective-permute-start | bytes 152 | tf_op jit(solution)/shard_map/ppermute | solution.py:186
  5.6 5.6 %collective-permute-start.2 = (s32[4,3]{1,0:T(4,128)}, s32[4,3]{1,0:T(4,128)S(1)}, u32[]{:S(2)}, u32[]{:S(2)}) collective-permute-start(s32[4,3]{1,0:T(4,128)} %refs_1_.1), channel_id=1, source_target_pairs={{0,24},{4,28},{8,16},{12,20},{16,8},{20,12},{24,0},{28,4},{1,25},{... | collective-permute-start | bytes 152 | tf_op jit(solution)/shard_map/ppermute | solution.py:186
  14.2 7.0 %collective-permute-start.12 = (bf16[4,64,128]{2,1,0:T(8,128)(2,1)S(1)}, bf16[4,64,128]{2,1,0:T(8,128)(2,1)S(1)}, u32[]{:S(2)}, u32[]{:S(2)}) collective-permute-start(bf16[4,64,128]{2,1,0:T(8,128)(2,1)S(1)} %get-tuple-element.42), channel_id=1, source_target_pairs={{0,16},{4,20},{8,24},{12,28},{16,0},{20,4},{24,8},{28,12},{1,17},{... | collective-permute-start | bytes 196616 | tf_op jit(solution)/shard_map/ppermute | solution.py:186
  16.4 6.2 %collective-permute-start.13 = (bf16[4,64,128]{2,1,0:T(8,128)(2,1)S(1)}, bf16[4,64,128]{2,1,0:T(8,128)(2,1)S(1)}, u32[]{:S(2)}, u32[]{:S(2)}) collective-permute-start(bf16[4,64,128]{2,1,0:T(8,128)(2,1)S(1)} %get-tuple-element.43), channel_id=1, source_target_pairs={{0,24},{4,28},{8,16},{12,20},{16,8},{20,12},{24,0},{28,4},{1,25},{... | collective-permute-start | bytes 196616 | tf_op jit(solution)/shard_map/ppermute | solution.py:186
  26.7 16.0 %collective-permute-start.17 = (bf16[8,128,128]{2,1,0:T(8,128)(2,1)S(1)}, bf16[8,128,128]{2,1,0:T(8,128)(2,1)S(1)}, u32[]{:S(2)}, u32[]{:S(2)}) collective-permute-start(bf16[8,128,128]{2,1,0:T(8,128)(2,1)S(1)} %get-tuple-element.48), channel_id=1, source_target_pairs={{0,3},{1,2},{2,1},{3,0},{4,7},{5,6},{6,5},{7,4},{8,11},{9,10},{10,... | collective-permute-start | bytes 786440 | tf_op jit(solution)/shard_map/ppermute | solution.py:189
  29.3 5.7 %collective-permute-start.5 = (bf16[4,64,128]{2,1,0:T(8,128)(2,1)S(1)}, bf16[4,64,128]{2,1,0:T(8,128)(2,1)S(1)}, u32[]{:S(2)}, u32[]{:S(2)}) collective-permute-start(bf16[4,64,128]{2,1,0:T(8,128)(2,1)S(1)} %get-tuple-element.33), channel_id=1, source_target_pairs={{0,16},{4,20},{8,24},{12,28},{16,0},{20,4},{24,8},{28,12},{1,17},{... | collective-permute-start | bytes 196616 | tf_op jit(solution)/shard_map/ppermute | solution.py:186
  32.0 6.1 %collective-permute-start.6 = (bf16[4,64,128]{2,1,0:T(8,128)(2,1)S(1)}, bf16[4,64,128]{2,1,0:T(8,128)(2,1)S(1)}, u32[]{:S(2)}, u32[]{:S(2)}) collective-permute-start(bf16[4,64,128]{2,1,0:T(8,128)(2,1)S(1)} %get-tuple-element.34), channel_id=1, source_target_pairs={{0,24},{4,28},{8,16},{12,20},{16,8},{20,12},{24,0},{28,4},{1,25},{... | collective-permute-start | bytes 196616 | tf_op jit(solution)/shard_map/ppermute | solution.py:186
  33.7 33.1 %collective-permute-start.14 = (bf16[16,128,128]{2,1,0:T(8,128)(2,1)S(1)}, bf16[16,128,128]{2,1,0:T(8,128)(2,1)S(1)}, u32[]{:S(2)}, u32[]{:S(2)}) collective-permute-start(bf16[16,128,128]{2,1,0:T(8,128)(2,1)S(1)} %get-tuple-element.45), channel_id=1, source_target_pairs={{0,1},{1,0},{2,3},{3,2},{4,5},{5,4},{6,7},{7,6},{8,9},{9,8},{10,11... | collective-permute-start | bytes 1572872 | tf_op jit(solution)/shard_map/ppermute | solution.py:189
  34.2 32.6 %collective-permute-start.15 = (bf16[16,128,128]{2,1,0:T(8,128)(2,1)S(1)}, bf16[16,128,128]{2,1,0:T(8,128)(2,1)S(1)}, u32[]{:S(2)}, u32[]{:S(2)}) collective-permute-start(bf16[16,128,128]{2,1,0:T(8,128)(2,1)S(1)} %get-tuple-element.46), channel_id=1, source_target_pairs={{0,2},{1,3},{2,0},{3,1},{4,6},{5,7},{6,4},{7,5},{8,10},{9,11},{10,... | collective-permute-start | bytes 1572872 | tf_op jit(solution)/shard_map/ppermute | solution.py:189
  35.0 19.1 %collective-permute-start.16 = (bf16[8,128,128]{2,1,0:T(8,128)(2,1)S(1)}, bf16[8,128,128]{2,1,0:T(8,128)(2,1)S(1)}, u32[]{:S(2)}, u32[]{:S(2)}) collective-permute-start(bf16[8,128,128]{2,1,0:T(8,128)(2,1)S(1)} %get-tuple-element.47), channel_id=1, source_target_pairs={{0,3},{1,2},{2,1},{3,0},{4,7},{5,6},{6,5},{7,4},{8,11},{9,10},{10,... | collective-permute-start | bytes 786440 | tf_op jit(solution)/shard_map/ppermute | solution.py:189
  42.2 17.5 %collective-permute-start.10 = (bf16[8,128,128]{2,1,0:T(8,128)(2,1)S(1)}, bf16[8,128,128]{2,1,0:T(8,128)(2,1)S(1)}, u32[]{:S(2)}, u32[]{:S(2)}) collective-permute-start(bf16[8,128,128]{2,1,0:T(8,128)(2,1)S(1)} %get-tuple-element.39), channel_id=1, source_target_pairs={{0,3},{1,2},{2,1},{3,0},{4,7},{5,6},{6,5},{7,4},{8,11},{9,10},{10,... | collective-permute-start | bytes 786440 | tf_op jit(solution)/shard_map/ppermute | solution.py:189
  42.7 22.6 %collective-permute-start.9 = (bf16[8,128,128]{2,1,0:T(8,128)(2,1)S(1)}, bf16[8,128,128]{2,1,0:T(8,128)(2,1)S(1)}, u32[]{:S(2)}, u32[]{:S(2)}) collective-permute-start(bf16[8,128,128]{2,1,0:T(8,128)(2,1)S(1)} %get-tuple-element.38), channel_id=1, source_target_pairs={{0,3},{1,2},{2,1},{3,0},{4,7},{5,6},{6,5},{7,4},{8,11},{9,10},{10,... | collective-permute-start | bytes 786440 | tf_op jit(solution)/shard_map/ppermute | solution.py:189
  54.2 14.9 %collective-permute-start.23 = (bf16[16,128,128]{2,1,0:T(8,128)(2,1)S(1)}, bf16[16,128,128]{2,1,0:T(8,128)(2,1)S(1)}, u32[]{:S(2)}, u32[]{:S(2)}) collective-permute-start(bf16[16,128,128]{2,1,0:T(8,128)(2,1)S(1)} %get-tuple-element.44.refs_1_), channel_id=1, source_target_pairs={{0,28},{4,0},{8,4},{12,8},{16,12},{20,16},{24,20},{28,24},{1,29},{... | collective-permute-start | bytes 1572872 | tf_op jit(solution)/shard_map/ppermute | solution.py:183
  59.7 17.5 %collective-permute-start.7 = (bf16[16,128,128]{2,1,0:T(8,128)(2,1)S(1)}, bf16[16,128,128]{2,1,0:T(8,128)(2,1)S(1)}, u32[]{:S(2)}, u32[]{:S(2)}) collective-permute-start(bf16[16,128,128]{2,1,0:T(8,128)(2,1)S(1)} %get-tuple-element.36), channel_id=1, source_target_pairs={{0,1},{1,0},{2,3},{3,2},{4,5},{5,4},{6,7},{7,6},{8,9},{9,8},{10,11... | collective-permute-start | bytes 1572872 | tf_op jit(solution)/shard_map/ppermute | solution.py:189
  65.3 11.9 %collective-permute-start.8 = (bf16[16,128,128]{2,1,0:T(8,128)(2,1)S(1)}, bf16[16,128,128]{2,1,0:T(8,128)(2,1)S(1)}, u32[]{:S(2)}, u32[]{:S(2)}) collective-permute-start(bf16[16,128,128]{2,1,0:T(8,128)(2,1)S(1)} %get-tuple-element.37), channel_id=1, source_target_pairs={{0,2},{1,3},{2,0},{3,1},{4,6},{5,7},{6,4},{7,5},{8,10},{9,11},{10,... | collective-permute-start | bytes 1572872 | tf_op jit(solution)/shard_map/ppermute | solution.py:189
  66.9 7.6 %collective-permute-start.26 = (bf16[8,128,128]{2,1,0:T(8,128)(2,1)S(1)}, bf16[8,128,128]{2,1,0:T(8,128)(2,1)S(1)}, u32[]{:S(2)}, u32[]{:S(2)}) collective-permute-start(bf16[8,128,128]{2,1,0:T(8,128)(2,1)S(1)} %collective-permute-done.16.refs_4_), channel_id=1, source_target_pairs={{0,28},{4,0},{8,4},{12,8},{16,12},{20,16},{24,20},{28,24},{1,29},{... | collective-permute-start | bytes 786440 | tf_op jit(solution)/shard_map/ppermute | solution.py:183
  69.0 30.8 %collective-permute-start.18 = (bf16[16,128,128]{2,1,0:T(8,128)(2,1)S(1)}, bf16[16,128,128]{2,1,0:T(8,128)(2,1)S(1)}, u32[]{:S(2)}, u32[]{:S(2)}) collective-permute-start(bf16[16,128,128]{2,1,0:T(8,128)(2,1)S(1)} %get-tuple-element.35.refs_1_), channel_id=1, source_target_pairs={{0,28},{4,0},{8,4},{12,8},{16,12},{20,16},{24,20},{28,24},{1,29},{... | collective-permute-start | bytes 1572872 | tf_op jit(solution)/shard_map/ppermute | solution.py:183
  70.7 14.0 %collective-permute-start.24 = (bf16[16,128,128]{2,1,0:T(8,128)(2,1)S(1)}, bf16[16,128,128]{2,1,0:T(8,128)(2,1)S(1)}, u32[]{:S(2)}, u32[]{:S(2)}) collective-permute-start(bf16[16,128,128]{2,1,0:T(8,128)(2,1)S(1)} %collective-permute-done.14.refs_2_), channel_id=1, source_target_pairs={{0,28},{4,0},{8,4},{12,8},{16,12},{20,16},{24,20},{28,24},{1,29},{... | collective-permute-start | bytes 1572872 | tf_op jit(solution)/shard_map/ppermute | solution.py:183
  74.4 16.0 %collective-permute-start.25 = (bf16[16,128,128]{2,1,0:T(8,128)(2,1)S(1)}, bf16[16,128,128]{2,1,0:T(8,128)(2,1)S(1)}, u32[]{:S(2)}, u32[]{:S(2)}) collective-permute-start(bf16[16,128,128]{2,1,0:T(8,128)(2,1)S(1)} %collective-permute-done.15.refs_3_), channel_id=1, source_target_pairs={{0,28},{4,0},{8,4},{12,8},{16,12},{20,16},{24,20},{28,24},{1,29},{... | collective-permute-start | bytes 1572872 | tf_op jit(solution)/shard_map/ppermute | solution.py:183
  77.3 27.2 %collective-permute-start.19 = (bf16[16,128,128]{2,1,0:T(8,128)(2,1)S(1)}, bf16[16,128,128]{2,1,0:T(8,128)(2,1)S(1)}, u32[]{:S(2)}, u32[]{:S(2)}) collective-permute-start(bf16[16,128,128]{2,1,0:T(8,128)(2,1)S(1)} %collective-permute-done.7.refs_2_), channel_id=1, source_target_pairs={{0,28},{4,0},{8,4},{12,8},{16,12},{20,16},{24,20},{28,24},{1,29},{... | collective-permute-start | bytes 1572872 | tf_op jit(solution)/shard_map/ppermute | solution.py:183
  77.3 27.2 %collective-permute-start.20 = (bf16[16,128,128]{2,1,0:T(8,128)(2,1)S(1)}, bf16[16,128,128]{2,1,0:T(8,128)(2,1)S(1)}, u32[]{:S(2)}, u32[]{:S(2)}) collective-permute-start(bf16[16,128,128]{2,1,0:T(8,128)(2,1)S(1)} %collective-permute-done.8.refs_3_), channel_id=1, source_target_pairs={{0,28},{4,0},{8,4},{12,8},{16,12},{20,16},{24,20},{28,24},{1,29},{... | collective-permute-start | bytes 1572872 | tf_op jit(solution)/shard_map/ppermute | solution.py:183
  84.8 19.7 %collective-permute-start.22 = (bf16[8,128,128]{2,1,0:T(8,128)(2,1)S(1)}, bf16[8,128,128]{2,1,0:T(8,128)(2,1)S(1)}, u32[]{:S(2)}, u32[]{:S(2)}) collective-permute-start(bf16[8,128,128]{2,1,0:T(8,128)(2,1)S(1)} %collective-permute-done.10.refs_4_), channel_id=1, source_target_pairs={{0,28},{4,0},{8,4},{12,8},{16,12},{20,16},{24,20},{28,24},{1,29},{... | collective-permute-start | bytes 786440 | tf_op jit(solution)/shard_map/ppermute | solution.py:183
  90.4 16.9 %collective-permute-start.21 = (bf16[8,128,128]{2,1,0:T(8,128)(2,1)S(1)}, bf16[8,128,128]{2,1,0:T(8,128)(2,1)S(1)}, u32[]{:S(2)}, u32[]{:S(2)}) collective-permute-start(bf16[8,128,128]{2,1,0:T(8,128)(2,1)S(1)} %collective-permute-done.9.refs_4_), channel_id=1, source_target_pairs={{0,28},{4,0},{8,4},{12,8},{16,12},{20,16},{24,20},{28,24},{1,29},{... | collective-permute-start | bytes 786440 | tf_op jit(solution)/shard_map/ppermute | solution.py:183
  (14 other events, 156.6 us)

commit v3 on v2

--- a/solution.py
+++ b/solution.py
@@ -8,8 +8,8 @@
 from jax.sharding import PartitionSpec as P
 
 
-PARTS = (1, 1)
-PIECES = (2, 2)
+PARTS = (3, 5)
+PIECES = ((1, 1), (3, 2))
 STEP_ROWS = 16
 GROUP = 4
 LONG = 20_000_000_000
@@ -218,8 +218,8 @@
         arrived = [given[c]]
         for chip in chips:
             arrived.append(same_core(given[chip * chunks + c], chip))
-        piece_rows = count // PIECES[c]
-        out_rows = [count] * last + [piece_rows] * PIECES[c]
+        piece_rows = [count * part // sum(PIECES[c]) for part in PIECES[c]]
+        out_rows = [count] * last + piece_rows
         halves = local_call(
             functools.partial(half_kernel, len(out_rows)),
             [jax.ShapeDtypeStruct((rows, block, block), bf16) for rows in out_rows],
@@ -233,17 +233,17 @@
             mine.append(across_aux(halves[away], away))
         for away in range(last):
             theirs.append(along_orb(mine[away], -1))
-        for j in range(PIECES[c]):
+        for j, rows in enumerate(piece_rows):
             mine_piece = across_aux(halves[last + j], last)
             their_piece = along_orb(mine_piece, -1)
-            pieces.append((c, j, piece_rows, mine + [mine_piece], theirs + [their_piece]))
+            pieces.append((c, j, sum(piece_rows[:j]), rows, mine + [mine_piece], theirs + [their_piece]))
 
     diagonal, coupling = [], []
     width = aux_count * block
-    for number, (c, j, count, mine, theirs) in enumerate(pieces):
+    for number, (c, j, first, count, mine, theirs) in enumerate(pieces):
         final = number == len(pieces) - 1
         fitted, *diagonal = local_call(
-            functools.partial(fit_kernel, aux_count, j * count),
+            functools.partial(fit_kernel, aux_count, first),
             [
                 jax.ShapeDtypeStruct((count, block, width), bf16),
                 jax.ShapeDtypeStruct((block, block), f32),
@@ -254,7 +254,7 @@
         )
         coupling = [
             local_call(
-                functools.partial(couple_kernel, aux_count, j * count, final),
+                functools.partial(couple_kernel, aux_count, first, final),
                 jax.ShapeDtypeStruct((block, 2 * block), bf16)
                 if final
                 else jax.ShapeDtypeStruct((block, block), f32),

time: 116 us -> 112 us (0.966)
  starting transfers between devices: 46 us -> 44.2 us
  waiting for transfers between devices: 50 us -> 48.5 us
    ppermute x9, waiting for transfers between devices: 10.6 us -> 5.52 us  [same_core(): return lax.ppermute(x, 'orb', [(i, i ^ 2 * chip) for i in range(orb_count)])]
    ppermute x11, waiting for transfers between devices: 22.4 us -> 25.7 us  [across_aux(): return lax.ppermute(x, 'aux', [(i, i ^ away) for i in range(aux_count)])]
    ppermute x11, starting transfers between devices: 15 us -> 12.7 us  [across_aux(): return lax.ppermute(x, 'aux', [(i, i ^ away) for i in range(aux_count)])]
  transfers between devices with their start and end apart: 31 -> 31, of which waited for: 17 -> 13; matrix products, arithmetic and copies ran while one was open for 0% -> 0% of each run, Pallas kernels for 9% -> 13%
where the time goes in v3:
time: 112 us
  waiting for transfers between devices  48.5 us (43%)
  starting transfers between devices  44.2 us (39%)
  Pallas kernels  16.5 us (15%)
  local copies, waits for them, and re-layouts  1.93 us (2%)
    ppermute x11, waiting for transfers between devices, across_aux(): return lax.ppermute(x, 'aux', [(i, i ^ away) for i in range(aux_count)])  25.7 us
    ppermute x10, waiting for transfers between devices, along_orb(): lax.ppermute(x, 'orb', [(i, (i + by) % orb_count) for i in range(orb_coun...  17.2 us
    ppermute x10, starting transfers between devices, along_orb(): lax.ppermute(x, 'orb', [(i, (i + by) % orb_count) for i in range(orb_coun...  17 us
    pallas_call x12, Pallas kernels, local_call(): pl.pallas_call(kernel, out_shape=out_shape, in_specs=[SMEM_SPEC] * len(sc...  16.5 us
    ppermute x9, starting transfers between devices, same_core(): return lax.ppermute(x, 'orb', [(i, i ^ 2 * chip) for i in range(orb_count)])  14 us
    ppermute x11, starting transfers between devices, across_aux(): return lax.ppermute(x, 'aux', [(i, i ^ away) for i in range(aux_count)])  12.7 us
    ppermute x9, waiting for transfers between devices, same_core(): return lax.ppermute(x, 'orb', [(i, i ^ 2 * chip) for i in range(orb_count)])  5.52 us
  transfers between devices with their start and end apart: 31, of which 13 were waited for; matrix products, arithmetic and copies ran while one was open for 0% of the time, Pallas kernels for 13%

profile of v3, /device:TPU:0, one launch (start us, length us, event | category | flops | bytes accessed | tf_op | source)
XLA Modules:
  0.0 112.0 jit_solution(11885735596840119859)
XLA Ops:
  0.5 2.6 %collective-permute-start = (s32[4,3]{1,0:T(4,128)}, s32[4,3]{1,0:T(4,128)S(1)}, u32[]{:S(2)}, u32[]{:S(2)}) collective-permute-start(s32[4,3]{1,0:T(4,128)} %refs_1_.1), channel_id=1, source_target_pairs={{0,8},{4,12},{8,0},{12,4},{16,24},{20,28},{24,16},{28,20},{1,9},{5... | collective-permute-start | bytes 152 | tf_op jit(solution)/shard_map/ppermute | solution.py:186
  3.1 2.6 %collective-permute-start.1 = (s32[4,3]{1,0:T(4,128)}, s32[4,3]{1,0:T(4,128)S(1)}, u32[]{:S(2)}, u32[]{:S(2)}) collective-permute-start(s32[4,3]{1,0:T(4,128)} %refs_1_.1), channel_id=1, source_target_pairs={{0,16},{4,20},{8,24},{12,28},{16,0},{20,4},{24,8},{28,12},{1,17},{... | collective-permute-start | bytes 152 | tf_op jit(solution)/shard_map/ppermute | solution.py:186
  5.7 2.0 %collective-permute-done.1.refs_3_ = s32[4,3]{1,0:T(4,128)S(1)} collective-permute-done((s32[4,3]{1,0:T(4,128)}, s32[4,3]{1,0:T(4,128)S(1)}, u32[]{:S(2)}, u32[]{:S(2)}) %collective-permute-start.1) | collective-permute-done | bytes 80 | tf_op jit(solution)/shard_map/ppermute | solution.py:186
  7.8 3.5 %collective-permute-done.2.refs_4_ = s32[4,3]{1,0:T(4,128)S(1)} collective-permute-done((s32[4,3]{1,0:T(4,128)}, s32[4,3]{1,0:T(4,128)S(1)}, u32[]{:S(2)}, u32[]{:S(2)}) %collective-permute-start.2) | collective-permute-done | bytes 80 | tf_op jit(solution)/shard_map/ppermute | solution.py:186
  14.3 2.1 %collective-permute-start.12 = (bf16[4,48,128]{2,1,0:T(8,128)(2,1)S(1)}, bf16[4,48,128]{2,1,0:T(8,128)(2,1)S(1)}, u32[]{:S(2)}, u32[]{:S(2)}) collective-permute-start(bf16[4,48,128]{2,1,0:T(8,128)(2,1)S(1)} %get-tuple-element.42), channel_id=1, source_target_pairs={{0,16},{4,20},{8,24},{12,28},{16,0},{20,4},{24,8},{28,12},{1,17},{... | collective-permute-start | bytes 147464 | tf_op jit(solution)/shard_map/ppermute | solution.py:186
  16.4 2.2 %collective-permute-start.13 = (bf16[4,48,128]{2,1,0:T(8,128)(2,1)S(1)}, bf16[4,48,128]{2,1,0:T(8,128)(2,1)S(1)}, u32[]{:S(2)}, u32[]{:S(2)}) collective-permute-start(bf16[4,48,128]{2,1,0:T(8,128)(2,1)S(1)} %get-tuple-element.43), channel_id=1, source_target_pairs={{0,24},{4,28},{8,16},{12,20},{16,8},{20,12},{24,0},{28,4},{1,25},{... | collective-permute-start | bytes 147464 | tf_op jit(solution)/shard_map/ppermute | solution.py:186
  18.7 2.2 %collective-permute-start.5 = (bf16[4,80,128]{2,1,0:T(8,128)(2,1)S(1)}, bf16[4,80,128]{2,1,0:T(8,128)(2,1)S(1)}, u32[]{:S(2)}, u32[]{:S(2)}) collective-permute-start(bf16[4,80,128]{2,1,0:T(8,128)(2,1)S(1)} %get-tuple-element.33), channel_id=1, source_target_pairs={{0,16},{4,20},{8,24},{12,28},{16,0},{20,4},{24,8},{28,12},{1,17},{... | collective-permute-start | bytes 245768 | tf_op jit(solution)/shard_map/ppermute | solution.py:186
  20.8 2.2 %collective-permute-start.6 = (bf16[4,80,128]{2,1,0:T(8,128)(2,1)S(1)}, bf16[4,80,128]{2,1,0:T(8,128)(2,1)S(1)}, u32[]{:S(2)}, u32[]{:S(2)}) collective-permute-start(bf16[4,80,128]{2,1,0:T(8,128)(2,1)S(1)} %get-tuple-element.34), channel_id=1, source_target_pairs={{0,24},{4,28},{8,16},{12,20},{16,8},{20,12},{24,0},{28,4},{1,25},{... | collective-permute-start | bytes 245768 | tf_op jit(solution)/shard_map/ppermute | solution.py:186
  23.1 4.0 %shard_map.49 = (bf16[12,128,128]{2,1,0:T(8,128)(2,1)S(1)}, bf16[12,128,128]{2,1,0:T(8,128)(2,1)S(1)}, bf16[12,128,128]{2,1,0:T(8,128)(2,1)S(1)}, bf16[6,128,128...) custom-call(bf16[4,128,128,128]{3,2,1,0:T(8,128)(2,1)S(1)} %bitcast.4, bf16[4,48,128]{2,1,0:T(8,128)(2,1)S(1)} %get-tuple-element.40.refs_1_, ...), custom_call_target="tpu_custom_call" | custom-call | flops 805306368 | bytes 1048576 | tf_op jit(solution)/shard_map/pallas_call | solution.py:24
  27.1 2.6 %collective-permute-start.17 = (bf16[6,128,128]{2,1,0:T(8,128)(2,1)S(1)}, bf16[6,128,128]{2,1,0:T(8,128)(2,1)S(1)}, u32[]{:S(2)}, u32[]{:S(2)}) collective-permute-start(bf16[6,128,128]{2,1,0:T(8,128)(2,1)S(1)} %get-tuple-element.48), channel_id=1, source_target_pairs={{0,3},{1,2},{2,1},{3,0},{4,7},{5,6},{6,5},{7,4},{8,11},{9,10},{10,... | collective-permute-start | bytes 589832 | tf_op jit(solution)/shard_map/ppermute | solution.py:189
  29.7 4.2 %shard_map.48 = (bf16[20,128,128]{2,1,0:T(8,128)(2,1)S(1)}, bf16[20,128,128]{2,1,0:T(8,128)(2,1)S(1)}, bf16[20,128,128]{2,1,0:T(8,128)(2,1)S(1)}, bf16[12,128,12...) custom-call(bf16[4,128,128,128]{3,2,1,0:T(8,128)(2,1)S(1)} %bitcast.4, bf16[4,80,128]{2,1,0:T(8,128)(2,1)S(1)} %get-tuple-element.31.refs_1_, ...), custom_call_target="tpu_custom_call" | custom-call | flops 1342177280 | bytes 1048576 | tf_op jit(solution)/shard_map/pallas_call | solution.py:24
  34.5 2.5 %collective-permute-start.16 = (bf16[6,128,128]{2,1,0:T(8,128)(2,1)S(1)}, bf16[6,128,128]{2,1,0:T(8,128)(2,1)S(1)}, u32[]{:S(2)}, u32[]{:S(2)}) collective-permute-start(bf16[6,128,128]{2,1,0:T(8,128)(2,1)S(1)} %get-tuple-element.47), channel_id=1, source_target_pairs={{0,3},{1,2},{2,1},{3,0},{4,7},{5,6},{6,5},{7,4},{8,11},{9,10},{10,... | collective-permute-start | bytes 589832 | tf_op jit(solution)/shard_map/ppermute | solution.py:189
  38.0 10.4 %collective-permute-done.16.refs_4_ = bf16[6,128,128]{2,1,0:T(8,128)(2,1)S(1)} collective-permute-done((bf16[6,128,128]{2,1,0:T(8,128)(2,1)S(1)}, bf16[6,128,128]{2,1,0:T(8,128)(2,1)S(1)}, u32[]{:S(2)}, u32[]{:S(2)}) %collective-permute-start.16) | collective-permute-done | bytes 196640 | tf_op jit(solution)/shard_map/ppermute | solution.py:189
  49.4 6.4 %collective-permute-done.14.refs_2_ = bf16[12,128,128]{2,1,0:T(8,128)(2,1)S(1)} collective-permute-done((bf16[12,128,128]{2,1,0:T(8,128)(2,1)S(1)}, bf16[12,128,128]{2,1,0:T(8,128)(2,1)S(1)}, u32[]{:S(2)}, u32[]{:S(2)}) %collective-permute-start.14) | collective-permute-done | bytes 393248 | tf_op jit(solution)/shard_map/ppermute | solution.py:189
  59.2 3.5 %collective-permute-start.26 = (bf16[6,128,128]{2,1,0:T(8,128)(2,1)S(1)}, bf16[6,128,128]{2,1,0:T(8,128)(2,1)S(1)}, u32[]{:S(2)}, u32[]{:S(2)}) collective-permute-start(bf16[6,128,128]{2,1,0:T(8,128)(2,1)S(1)} %collective-permute-done.16.refs_4_), channel_id=1, source_target_pairs={{0,28},{4,0},{8,4},{12,8},{16,12},{20,16},{24,20},{28,24},{1,29},{... | collective-permute-start | bytes 589832 | tf_op jit(solution)/shard_map/ppermute | solution.py:183
  62.7 3.9 %collective-permute-done.26.refs_4_ = bf16[6,128,128]{2,1,0:T(8,128)(2,1)S(1)} collective-permute-done((bf16[6,128,128]{2,1,0:T(8,128)(2,1)S(1)}, bf16[6,128,128]{2,1,0:T(8,128)(2,1)S(1)}, u32[]{:S(2)}, u32[]{:S(2)}) %collective-permute-start.26) | collective-permute-done | bytes 196640 | tf_op jit(solution)/shard_map/ppermute | solution.py:183
  66.6 3.7 %collective-permute-start.18 = (bf16[20,128,128]{2,1,0:T(8,128)(2,1)S(1)}, bf16[20,128,128]{2,1,0:T(8,128)(2,1)S(1)}, u32[]{:S(2)}, u32[]{:S(2)}) collective-permute-start(bf16[20,128,128]{2,1,0:T(8,128)(2,1)S(1)} %get-tuple-element.35.refs_1_), channel_id=1, source_target_pairs={{0,28},{4,0},{8,4},{12,8},{16,12},{20,16},{24,20},{28,24},{1,29},{... | collective-permute-start | bytes 1966088 | tf_op jit(solution)/shard_map/ppermute | solution.py:183
  70.3 5.2 %collective-permute-done.10.refs_4_ = bf16[12,128,128]{2,1,0:T(8,128)(2,1)S(1)} collective-permute-done((bf16[12,128,128]{2,1,0:T(8,128)(2,1)S(1)}, bf16[12,128,128]{2,1,0:T(8,128)(2,1)S(1)}, u32[]{:S(2)}, u32[]{:S(2)}) %collective-permute-start.10) | collective-permute-done | bytes 393248 | tf_op jit(solution)/shard_map/ppermute | solution.py:189
  75.5 1.9 %collective-permute-start.22 = (bf16[12,128,128]{2,1,0:T(8,128)(2,1)S(1)}, bf16[12,128,128]{2,1,0:T(8,128)(2,1)S(1)}, u32[]{:S(2)}, u32[]{:S(2)}) collective-permute-start(bf16[12,128,128]{2,1,0:T(8,128)(2,1)S(1)} %collective-permute-done.10.refs_4_), channel_id=1, source_target_pairs={{0,28},{4,0},{8,4},{12,8},{16,12},{20,16},{24,20},{28,24},{1,29},{... | collective-permute-start | bytes 1179656 | tf_op jit(solution)/shard_map/ppermute | solution.py:183
  77.5 2.3 %collective-permute-start.20 = (bf16[20,128,128]{2,1,0:T(8,128)(2,1)S(1)}, bf16[20,128,128]{2,1,0:T(8,128)(2,1)S(1)}, u32[]{:S(2)}, u32[]{:S(2)}) collective-permute-start(bf16[20,128,128]{2,1,0:T(8,128)(2,1)S(1)} %collective-permute-done.8.refs_3_), channel_id=1, source_target_pairs={{0,28},{4,0},{8,4},{12,8},{16,12},{20,16},{24,20},{28,24},{1,29},{... | collective-permute-start | bytes 1966088 | tf_op jit(solution)/shard_map/ppermute | solution.py:183
  80.5 2.1 %collective-permute-done.25.refs_3_ = bf16[12,128,128]{2,1,0:T(8,128)(2,1)S(1)} collective-permute-done((bf16[12,128,128]{2,1,0:T(8,128)(2,1)S(1)}, bf16[12,128,128]{2,1,0:T(8,128)(2,1)S(1)}, u32[]{:S(2)}, u32[]{:S(2)}) %collective-permute-start.25) | collective-permute-done | bytes 393248 | tf_op jit(solution)/shard_map/ppermute | solution.py:183
  82.6 3.7 %collective-permute-start.21 = (bf16[8,128,128]{2,1,0:T(8,128)(2,1)S(1)}, bf16[8,128,128]{2,1,0:T(8,128)(2,1)S(1)}, u32[]{:S(2)}, u32[]{:S(2)}) collective-permute-start(bf16[8,128,128]{2,1,0:T(8,128)(2,1)S(1)} %collective-permute-done.9.refs_4_), channel_id=1, source_target_pairs={{0,28},{4,0},{8,4},{12,8},{16,12},{20,16},{24,20},{28,24},{1,29},{... | collective-permute-start | bytes 786440 | tf_op jit(solution)/shard_map/ppermute | solution.py:183
  93.8 7.0 %collective-permute-done.20.refs_3_ = bf16[20,128,128]{2,1,0:T(8,128)(2,1)S(1)} collective-permute-done((bf16[20,128,128]{2,1,0:T(8,128)(2,1)S(1)}, bf16[20,128,128]{2,1,0:T(8,128)(2,1)S(1)}, u32[]{:S(2)}, u32[]{:S(2)}) %collective-permute-start.20) | collective-permute-done | bytes 655392 | tf_op jit(solution)/shard_map/ppermute | solution.py:183
  101.4 2.2 %collective-permute-done.21.refs_4_ = bf16[8,128,128]{2,1,0:T(8,128)(2,1)S(1)} collective-permute-done((bf16[8,128,128]{2,1,0:T(8,128)(2,1)S(1)}, bf16[8,128,128]{2,1,0:T(8,128)(2,1)S(1)}, u32[]{:S(2)}, u32[]{:S(2)}) %collective-permute-start.21) | collective-permute-done | bytes 262176 | tf_op jit(solution)/shard_map/ppermute | solution.py:183
  (67 shorter events, 26.7 us)
Async XLA Ops:
  0.0 11.2 %collective-permute-start.3 = (bf16[4096,128]{1,0:T(8,128)(2,1)}, bf16[4096,128]{1,0:T(8,128)(2,1)S(1)}, u32[]{:S(2)}, u32[]{:S(2)}) collective-permute-start(bf16[4096,128]{1,0:T(8,128)(2,1)} %refs_5_.1), channel_id=1, source_target_pairs={{0,4},{4,0},{8,12},{12,8},{16,20},{20,16},{24,28},{28,24},{1,5},{5... | collective-permute-start | bytes 3145736 | tf_op jit(solution)/shard_map/ppermute | solution.py:198
  14.2 6.6 %collective-permute-start.11 = (bf16[4,48,128]{2,1,0:T(8,128)(2,1)S(1)}, bf16[4,48,128]{2,1,0:T(8,128)(2,1)S(1)}, u32[]{:S(2)}, u32[]{:S(2)}) collective-permute-start(bf16[4,48,128]{2,1,0:T(8,128)(2,1)S(1)} %get-tuple-element.41), channel_id=1, source_target_pairs={{0,8},{4,12},{8,0},{12,4},{16,24},{20,28},{24,16},{28,20},{1,9},{5... | collective-permute-start | bytes 147464 | tf_op jit(solution)/shard_map/ppermute | solution.py:186
  14.3 8.8 %collective-permute-start.12 = (bf16[4,48,128]{2,1,0:T(8,128)(2,1)S(1)}, bf16[4,48,128]{2,1,0:T(8,128)(2,1)S(1)}, u32[]{:S(2)}, u32[]{:S(2)}) collective-permute-start(bf16[4,48,128]{2,1,0:T(8,128)(2,1)S(1)} %get-tuple-element.42), channel_id=1, source_target_pairs={{0,16},{4,20},{8,24},{12,28},{16,0},{20,4},{24,8},{28,12},{1,17},{... | collective-permute-start | bytes 147464 | tf_op jit(solution)/shard_map/ppermute | solution.py:186
  16.4 6.6 %collective-permute-start.13 = (bf16[4,48,128]{2,1,0:T(8,128)(2,1)S(1)}, bf16[4,48,128]{2,1,0:T(8,128)(2,1)S(1)}, u32[]{:S(2)}, u32[]{:S(2)}) collective-permute-start(bf16[4,48,128]{2,1,0:T(8,128)(2,1)S(1)} %get-tuple-element.43), channel_id=1, source_target_pairs={{0,24},{4,28},{8,16},{12,20},{16,8},{20,12},{24,0},{28,4},{1,25},{... | collective-permute-start | bytes 147464 | tf_op jit(solution)/shard_map/ppermute | solution.py:186
  18.7 11.0 %collective-permute-start.4 = (bf16[4,80,128]{2,1,0:T(8,128)(2,1)S(1)}, bf16[4,80,128]{2,1,0:T(8,128)(2,1)S(1)}, u32[]{:S(2)}, u32[]{:S(2)}) collective-permute-start(bf16[4,80,128]{2,1,0:T(8,128)(2,1)S(1)} %get-tuple-element.32), channel_id=1, source_target_pairs={{0,8},{4,12},{8,0},{12,4},{16,24},{20,28},{24,16},{28,20},{1,9},{5... | collective-permute-start | bytes 245768 | tf_op jit(solution)/shard_map/ppermute | solution.py:186
  18.7 11.0 %collective-permute-start.5 = (bf16[4,80,128]{2,1,0:T(8,128)(2,1)S(1)}, bf16[4,80,128]{2,1,0:T(8,128)(2,1)S(1)}, u32[]{:S(2)}, u32[]{:S(2)}) collective-permute-start(bf16[4,80,128]{2,1,0:T(8,128)(2,1)S(1)} %get-tuple-element.33), channel_id=1, source_target_pairs={{0,16},{4,20},{8,24},{12,28},{16,0},{20,4},{24,8},{28,12},{1,17},{... | collective-permute-start | bytes 245768 | tf_op jit(solution)/shard_map/ppermute | solution.py:186
  20.8 8.9 %collective-permute-start.6 = (bf16[4,80,128]{2,1,0:T(8,128)(2,1)S(1)}, bf16[4,80,128]{2,1,0:T(8,128)(2,1)S(1)}, u32[]{:S(2)}, u32[]{:S(2)}) collective-permute-start(bf16[4,80,128]{2,1,0:T(8,128)(2,1)S(1)} %get-tuple-element.34), channel_id=1, source_target_pairs={{0,24},{4,28},{8,16},{12,20},{16,8},{20,12},{24,0},{28,4},{1,25},{... | collective-permute-start | bytes 245768 | tf_op jit(solution)/shard_map/ppermute | solution.py:186
  27.1 10.8 %collective-permute-start.17 = (bf16[6,128,128]{2,1,0:T(8,128)(2,1)S(1)}, bf16[6,128,128]{2,1,0:T(8,128)(2,1)S(1)}, u32[]{:S(2)}, u32[]{:S(2)}) collective-permute-start(bf16[6,128,128]{2,1,0:T(8,128)(2,1)S(1)} %get-tuple-element.48), channel_id=1, source_target_pairs={{0,3},{1,2},{2,1},{3,0},{4,7},{5,6},{6,5},{7,4},{8,11},{9,10},{10,... | collective-permute-start | bytes 589832 | tf_op jit(solution)/shard_map/ppermute | solution.py:189
  34.0 14.9 %collective-permute-start.9 = (bf16[8,128,128]{2,1,0:T(8,128)(2,1)S(1)}, bf16[8,128,128]{2,1,0:T(8,128)(2,1)S(1)}, u32[]{:S(2)}, u32[]{:S(2)}) collective-permute-start(bf16[8,128,128]{2,1,0:T(8,128)(2,1)S(1)} %get-tuple-element.38), channel_id=1, source_target_pairs={{0,3},{1,2},{2,1},{3,0},{4,7},{5,6},{6,5},{7,4},{8,11},{9,10},{10,... | collective-permute-start | bytes 786440 | tf_op jit(solution)/shard_map/ppermute | solution.py:189
  34.5 13.9 %collective-permute-start.16 = (bf16[6,128,128]{2,1,0:T(8,128)(2,1)S(1)}, bf16[6,128,128]{2,1,0:T(8,128)(2,1)S(1)}, u32[]{:S(2)}, u32[]{:S(2)}) collective-permute-start(bf16[6,128,128]{2,1,0:T(8,128)(2,1)S(1)} %get-tuple-element.47), channel_id=1, source_target_pairs={{0,3},{1,2},{2,1},{3,0},{4,7},{5,6},{6,5},{7,4},{8,11},{9,10},{10,... | collective-permute-start | bytes 589832 | tf_op jit(solution)/shard_map/ppermute | solution.py:189
  36.9 18.8 %collective-permute-start.14 = (bf16[12,128,128]{2,1,0:T(8,128)(2,1)S(1)}, bf16[12,128,128]{2,1,0:T(8,128)(2,1)S(1)}, u32[]{:S(2)}, u32[]{:S(2)}) collective-permute-start(bf16[12,128,128]{2,1,0:T(8,128)(2,1)S(1)} %get-tuple-element.45), channel_id=1, source_target_pairs={{0,1},{1,0},{2,3},{3,2},{4,5},{5,4},{6,7},{7,6},{8,9},{9,8},{10,11... | collective-permute-start | bytes 1179656 | tf_op jit(solution)/shard_map/ppermute | solution.py:189
  37.5 18.3 %collective-permute-start.15 = (bf16[12,128,128]{2,1,0:T(8,128)(2,1)S(1)}, bf16[12,128,128]{2,1,0:T(8,128)(2,1)S(1)}, u32[]{:S(2)}, u32[]{:S(2)}) collective-permute-start(bf16[12,128,128]{2,1,0:T(8,128)(2,1)S(1)} %get-tuple-element.46), channel_id=1, source_target_pairs={{0,2},{1,3},{2,0},{3,1},{4,6},{5,7},{6,4},{7,5},{8,10},{9,11},{10,... | collective-permute-start | bytes 1179656 | tf_op jit(solution)/shard_map/ppermute | solution.py:189
  37.9 19.4 %collective-permute-start.23 = (bf16[12,128,128]{2,1,0:T(8,128)(2,1)S(1)}, bf16[12,128,128]{2,1,0:T(8,128)(2,1)S(1)}, u32[]{:S(2)}, u32[]{:S(2)}) collective-permute-start(bf16[12,128,128]{2,1,0:T(8,128)(2,1)S(1)} %get-tuple-element.44.refs_1_), channel_id=1, source_target_pairs={{0,28},{4,0},{8,4},{12,8},{16,12},{20,16},{24,20},{28,24},{1,29},{... | collective-permute-start | bytes 1179656 | tf_op jit(solution)/shard_map/ppermute | solution.py:183
  48.3 27.2 %collective-permute-start.7 = (bf16[20,128,128]{2,1,0:T(8,128)(2,1)S(1)}, bf16[20,128,128]{2,1,0:T(8,128)(2,1)S(1)}, u32[]{:S(2)}, u32[]{:S(2)}) collective-permute-start(bf16[20,128,128]{2,1,0:T(8,128)(2,1)S(1)} %get-tuple-element.36), channel_id=1, source_target_pairs={{0,1},{1,0},{2,3},{3,2},{4,5},{5,4},{6,7},{7,6},{8,9},{9,8},{10,11... | collective-permute-start | bytes 1966088 | tf_op jit(solution)/shard_map/ppermute | solution.py:189
  48.9 28.5 %collective-permute-start.8 = (bf16[20,128,128]{2,1,0:T(8,128)(2,1)S(1)}, bf16[20,128,128]{2,1,0:T(8,128)(2,1)S(1)}, u32[]{:S(2)}, u32[]{:S(2)}) collective-permute-start(bf16[20,128,128]{2,1,0:T(8,128)(2,1)S(1)} %get-tuple-element.37), channel_id=1, source_target_pairs={{0,2},{1,3},{2,0},{3,1},{4,6},{5,7},{6,4},{7,5},{8,10},{9,11},{10,... | collective-permute-start | bytes 1966088 | tf_op jit(solution)/shard_map/ppermute | solution.py:189
  55.8 19.7 %collective-permute-start.10 = (bf16[12,128,128]{2,1,0:T(8,128)(2,1)S(1)}, bf16[12,128,128]{2,1,0:T(8,128)(2,1)S(1)}, u32[]{:S(2)}, u32[]{:S(2)}) collective-permute-start(bf16[12,128,128]{2,1,0:T(8,128)(2,1)S(1)} %get-tuple-element.39), channel_id=1, source_target_pairs={{0,3},{1,2},{2,1},{3,0},{4,7},{5,6},{6,5},{7,4},{8,11},{9,10},{10,... | collective-permute-start | bytes 1179656 | tf_op jit(solution)/shard_map/ppermute | solution.py:189
  57.3 20.2 %collective-permute-start.24 = (bf16[12,128,128]{2,1,0:T(8,128)(2,1)S(1)}, bf16[12,128,128]{2,1,0:T(8,128)(2,1)S(1)}, u32[]{:S(2)}, u32[]{:S(2)}) collective-permute-start(bf16[12,128,128]{2,1,0:T(8,128)(2,1)S(1)} %collective-permute-done.14.refs_2_), channel_id=1, source_target_pairs={{0,28},{4,0},{8,4},{12,8},{16,12},{20,16},{24,20},{28,24},{1,29},{... | collective-permute-start | bytes 1179656 | tf_op jit(solution)/shard_map/ppermute | solution.py:183
  59.2 7.4 %collective-permute-start.26 = (bf16[6,128,128]{2,1,0:T(8,128)(2,1)S(1)}, bf16[6,128,128]{2,1,0:T(8,128)(2,1)S(1)}, u32[]{:S(2)}, u32[]{:S(2)}) collective-permute-start(bf16[6,128,128]{2,1,0:T(8,128)(2,1)S(1)} %collective-permute-done.16.refs_4_), channel_id=1, source_target_pairs={{0,28},{4,0},{8,4},{12,8},{16,12},{20,16},{24,20},{28,24},{1,29},{... | collective-permute-start | bytes 589832 | tf_op jit(solution)/shard_map/ppermute | solution.py:183
  66.6 25.3 %collective-permute-start.18 = (bf16[20,128,128]{2,1,0:T(8,128)(2,1)S(1)}, bf16[20,128,128]{2,1,0:T(8,128)(2,1)S(1)}, u32[]{:S(2)}, u32[]{:S(2)}) collective-permute-start(bf16[20,128,128]{2,1,0:T(8,128)(2,1)S(1)} %get-tuple-element.35.refs_1_), channel_id=1, source_target_pairs={{0,28},{4,0},{8,4},{12,8},{16,12},{20,16},{24,20},{28,24},{1,29},{... | collective-permute-start | bytes 1966088 | tf_op jit(solution)/shard_map/ppermute | solution.py:183
  75.5 7.1 %collective-permute-start.25 = (bf16[12,128,128]{2,1,0:T(8,128)(2,1)S(1)}, bf16[12,128,128]{2,1,0:T(8,128)(2,1)S(1)}, u32[]{:S(2)}, u32[]{:S(2)}) collective-permute-start(bf16[12,128,128]{2,1,0:T(8,128)(2,1)S(1)} %collective-permute-done.15.refs_3_), channel_id=1, source_target_pairs={{0,28},{4,0},{8,4},{12,8},{16,12},{20,16},{24,20},{28,24},{1,29},{... | collective-permute-start | bytes 1179656 | tf_op jit(solution)/shard_map/ppermute | solution.py:183
  75.5 16.4 %collective-permute-start.22 = (bf16[12,128,128]{2,1,0:T(8,128)(2,1)S(1)}, bf16[12,128,128]{2,1,0:T(8,128)(2,1)S(1)}, u32[]{:S(2)}, u32[]{:S(2)}) collective-permute-start(bf16[12,128,128]{2,1,0:T(8,128)(2,1)S(1)} %collective-permute-done.10.refs_4_), channel_id=1, source_target_pairs={{0,28},{4,0},{8,4},{12,8},{16,12},{20,16},{24,20},{28,24},{1,29},{... | collective-permute-start | bytes 1179656 | tf_op jit(solution)/shard_map/ppermute | solution.py:183
  77.4 16.4 %collective-permute-start.19 = (bf16[20,128,128]{2,1,0:T(8,128)(2,1)S(1)}, bf16[20,128,128]{2,1,0:T(8,128)(2,1)S(1)}, u32[]{:S(2)}, u32[]{:S(2)}) collective-permute-start(bf16[20,128,128]{2,1,0:T(8,128)(2,1)S(1)} %collective-permute-done.7.refs_2_), channel_id=1, source_target_pairs={{0,28},{4,0},{8,4},{12,8},{16,12},{20,16},{24,20},{28,24},{1,29},{... | collective-permute-start | bytes 1966088 | tf_op jit(solution)/shard_map/ppermute | solution.py:183
  77.5 23.4 %collective-permute-start.20 = (bf16[20,128,128]{2,1,0:T(8,128)(2,1)S(1)}, bf16[20,128,128]{2,1,0:T(8,128)(2,1)S(1)}, u32[]{:S(2)}, u32[]{:S(2)}) collective-permute-start(bf16[20,128,128]{2,1,0:T(8,128)(2,1)S(1)} %collective-permute-done.8.refs_3_), channel_id=1, source_target_pairs={{0,28},{4,0},{8,4},{12,8},{16,12},{20,16},{24,20},{28,24},{1,29},{... | collective-permute-start | bytes 1966088 | tf_op jit(solution)/shard_map/ppermute | solution.py:183
  82.6 21.1 %collective-permute-start.21 = (bf16[8,128,128]{2,1,0:T(8,128)(2,1)S(1)}, bf16[8,128,128]{2,1,0:T(8,128)(2,1)S(1)}, u32[]{:S(2)}, u32[]{:S(2)}) collective-permute-start(bf16[8,128,128]{2,1,0:T(8,128)(2,1)S(1)} %collective-permute-done.9.refs_4_), channel_id=1, source_target_pairs={{0,28},{4,0},{8,4},{12,8},{16,12},{20,16},{24,20},{28,24},{1,29},{... | collective-permute-start | bytes 786440 | tf_op jit(solution)/shard_map/ppermute | solution.py:183
  (14 other events, 160.8 us)

commit v4 on v3

--- a/solution.py
+++ b/solution.py
@@ -9,7 +9,7 @@
 
 
 PARTS = (3, 5)
-PIECES = ((1, 1), (3, 2))
+PIECES = ((1,), (2, 2, 1))
 STEP_ROWS = 16
 GROUP = 4
 LONG = 20_000_000_000
@@ -152,16 +152,16 @@
 
 
 def couple_kernel(aux_count, first, final, *refs):
-    total = gram([refs[0][i] for i in range(refs[0].shape[0])], refs[1 : 1 + aux_count], first)
-    before = refs[1 + aux_count : -1]
+    parts, before = refs[1 : 1 + aux_count], refs[1 + aux_count : -1]
+    total = gram([refs[0][i] for i in range(refs[0].shape[0])], parts, first)
     if final:
         before, diagonal = before[:-1], before[-1]
     for ref in before:
         total = total + ref[...]
     if final:
         block = total.shape[0]
-        refs[-1][:, :block] = diagonal[...].astype(jnp.bfloat16)
-        refs[-1][:, block:] = total.astype(jnp.bfloat16)
+        refs[-1][:, :block] = diagonal[...].astype(refs[-1].dtype)
+        refs[-1][:, block:] = total.astype(refs[-1].dtype)
     else:
         refs[-1][...] = total
 
@@ -179,8 +179,8 @@
     aux = lax.axis_index("aux")
     place = jnp.stack([(orb >> 1) * (2 * owned), orb & 1, aux]).astype(jnp.int32)
 
-    def along_orb(x, by):
-        return lax.ppermute(x, "orb", [(i, (i + by) % orb_count) for i in range(orb_count)])
+    def to_previous(x):
+        return lax.ppermute(x, "orb", [(i, (i - 1) % orb_count) for i in range(orb_count)])
 
     def same_core(x, chip):
         return lax.ppermute(x, "orb", [(i, i ^ (2 * chip)) for i in range(orb_count)])
@@ -232,10 +232,10 @@
         for away in range(1, last):
             mine.append(across_aux(halves[away], away))
         for away in range(last):
-            theirs.append(along_orb(mine[away], -1))
+            theirs.append(to_previous(mine[away]))
         for j, rows in enumerate(piece_rows):
             mine_piece = across_aux(halves[last + j], last)
-            their_piece = along_orb(mine_piece, -1)
+            their_piece = to_previous(mine_piece)
             pieces.append((c, j, sum(piece_rows[:j]), rows, mine + [mine_piece], theirs + [their_piece]))
 
     diagonal, coupling = [], []

time: 112 us -> 114 us (1.018)
  waiting for transfers between devices: 48.5 us -> 53.3 us
  starting transfers between devices: 44.2 us -> 41.5 us
    ppermute x9, waiting for transfers between devices: 5.52 us -> 13.9 us  [same_core(): return lax.ppermute(x, 'orb', [(i, i ^ 2 * chip) for i in range(orb_count)])]
    ppermute x10, starting transfers between devices: 17 us -> 13.4 us  [to_previous(): lax.ppermute(x, 'orb', [(i, (i - 1) % orb_count) for i in range(orb_count)])]
    ppermute x11, waiting for transfers between devices: 25.7 us -> 23.7 us  [across_aux(): return lax.ppermute(x, 'aux', [(i, i ^ away) for i in range(aux_count)])]
    ppermute x10, waiting for transfers between devices: 17.2 us -> 15.7 us  [to_previous(): lax.ppermute(x, 'orb', [(i, (i - 1) % orb_count) for i in range(orb_count)])]
  transfers between devices with their start and end apart: 31 -> 31, of which waited for: 13 -> 20; matrix products, arithmetic and copies ran while one was open for 0% -> 0% of each run, Pallas kernels for 13% -> 10%
where the time goes in v4:
time: 114 us
  waiting for transfers between devices  53.3 us (47%)
  starting transfers between devices  41.5 us (36%)
  Pallas kernels  16.5 us (14%)
  local copies, waits for them, and re-layouts  1.93 us (2%)
    ppermute x11, waiting for transfers between devices, across_aux(): return lax.ppermute(x, 'aux', [(i, i ^ away) for i in range(aux_count)])  23.7 us
    pallas_call x12, Pallas kernels, local_call(): pl.pallas_call(kernel, out_shape=out_shape, in_specs=[SMEM_SPEC] * len(sc...  16.5 us
    ppermute x10, waiting for transfers between devices, to_previous(): lax.ppermute(x, 'orb', [(i, (i - 1) % orb_count) for i in range(orb_count)])  15.7 us
    ppermute x9, starting transfers between devices, same_core(): return lax.ppermute(x, 'orb', [(i, i ^ 2 * chip) for i in range(orb_count)])  14 us
    ppermute x9, waiting for transfers between devices, same_core(): return lax.ppermute(x, 'orb', [(i, i ^ 2 * chip) for i in range(orb_count)])  13.9 us
    ppermute x11, starting transfers between devices, across_aux(): return lax.ppermute(x, 'aux', [(i, i ^ away) for i in range(aux_count)])  13.6 us
    ppermute x10, starting transfers between devices, to_previous(): lax.ppermute(x, 'orb', [(i, (i - 1) % orb_count) for i in range(orb_count)])  13.4 us
  transfers between devices with their start and end apart: 31, of which 20 were waited for; matrix products, arithmetic and copies ran while one was open for 0% of the time, Pallas kernels for 10%

profile of v4, /device:TPU:0, one launch (start us, length us, event | category | flops | bytes accessed | tf_op | source)
XLA Modules:
  0.0 114.1 jit_solution(9367706413499803145)
XLA Ops:
  0.5 2.6 %collective-permute-start = (s32[4,3]{1,0:T(4,128)}, s32[4,3]{1,0:T(4,128)S(1)}, u32[]{:S(2)}, u32[]{:S(2)}) collective-permute-start(s32[4,3]{1,0:T(4,128)} %refs_1_.1), channel_id=1, source_target_pairs={{0,8},{4,12},{8,0},{12,4},{16,24},{20,28},{24,16},{28,20},{1,9},{5... | collective-permute-start | bytes 152 | tf_op jit(solution)/shard_map/ppermute | solution.py:186
  3.1 2.6 %collective-permute-start.1 = (s32[4,3]{1,0:T(4,128)}, s32[4,3]{1,0:T(4,128)S(1)}, u32[]{:S(2)}, u32[]{:S(2)}) collective-permute-start(s32[4,3]{1,0:T(4,128)} %refs_1_.1), channel_id=1, source_target_pairs={{0,16},{4,20},{8,24},{12,28},{16,0},{20,4},{24,8},{28,12},{1,17},{... | collective-permute-start | bytes 152 | tf_op jit(solution)/shard_map/ppermute | solution.py:186
  5.7 2.0 %collective-permute-done.1.refs_3_ = s32[4,3]{1,0:T(4,128)S(1)} collective-permute-done((s32[4,3]{1,0:T(4,128)}, s32[4,3]{1,0:T(4,128)S(1)}, u32[]{:S(2)}, u32[]{:S(2)}) %collective-permute-start.1) | collective-permute-done | bytes 80 | tf_op jit(solution)/shard_map/ppermute | solution.py:186
  7.8 3.5 %collective-permute-done.2.refs_4_ = s32[4,3]{1,0:T(4,128)S(1)} collective-permute-done((s32[4,3]{1,0:T(4,128)}, s32[4,3]{1,0:T(4,128)S(1)}, u32[]{:S(2)}, u32[]{:S(2)}) %collective-permute-start.2) | collective-permute-done | bytes 80 | tf_op jit(solution)/shard_map/ppermute | solution.py:186
  14.3 2.1 %collective-permute-start.5 = (bf16[4,80,128]{2,1,0:T(8,128)(2,1)S(1)}, bf16[4,80,128]{2,1,0:T(8,128)(2,1)S(1)}, u32[]{:S(2)}, u32[]{:S(2)}) collective-permute-start(bf16[4,80,128]{2,1,0:T(8,128)(2,1)S(1)} %get-tuple-element.33), channel_id=1, source_target_pairs={{0,16},{4,20},{8,24},{12,28},{16,0},{20,4},{24,8},{28,12},{1,17},{... | collective-permute-start | bytes 245768 | tf_op jit(solution)/shard_map/ppermute | solution.py:186
  16.4 2.2 %collective-permute-start.6 = (bf16[4,80,128]{2,1,0:T(8,128)(2,1)S(1)}, bf16[4,80,128]{2,1,0:T(8,128)(2,1)S(1)}, u32[]{:S(2)}, u32[]{:S(2)}) collective-permute-start(bf16[4,80,128]{2,1,0:T(8,128)(2,1)S(1)} %get-tuple-element.34), channel_id=1, source_target_pairs={{0,24},{4,28},{8,16},{12,20},{16,8},{20,12},{24,0},{28,4},{1,25},{... | collective-permute-start | bytes 245768 | tf_op jit(solution)/shard_map/ppermute | solution.py:186
  18.8 4.4 %collective-permute-done.5.refs_3_ = bf16[4,80,128]{2,1,0:T(8,128)(2,1)S(1)} collective-permute-done((bf16[4,80,128]{2,1,0:T(8,128)(2,1)S(1)}, bf16[4,80,128]{2,1,0:T(8,128)(2,1)S(1)}, u32[]{:S(2)}, u32[]{:S(2)}) %collective-permute-start.5) | collective-permute-done | bytes 81952 | tf_op jit(solution)/shard_map/ppermute | solution.py:186
  23.2 4.2 %shard_map.48 = (bf16[20,128,128]{2,1,0:T(8,128)(2,1)S(1)}, bf16[20,128,128]{2,1,0:T(8,128)(2,1)S(1)}, bf16[20,128,128]{2,1,0:T(8,128)(2,1)S(1)}, bf16[8,128,128...) custom-call(bf16[4,128,128,128]{3,2,1,0:T(8,128)(2,1)S(1)} %bitcast.4, ...), custom_call_target="tpu_custom_call" | custom-call | flops 1342177280 | bytes 1048576 | tf_op jit(solution)/shard_map/pallas_call | solution.py:24
  27.5 2.5 %collective-permute-start.11 = (bf16[8,128,128]{2,1,0:T(8,128)(2,1)S(1)}, bf16[8,128,128]{2,1,0:T(8,128)(2,1)S(1)}, u32[]{:S(2)}, u32[]{:S(2)}) collective-permute-start(bf16[8,128,128]{2,1,0:T(8,128)(2,1)S(1)} %get-tuple-element.40), channel_id=1, source_target_pairs={{0,3},{1,2},{2,1},{3,0},{4,7},{5,6},{6,5},{7,4},{8,11},{9,10},{10,... | collective-permute-start | bytes 786440 | tf_op jit(solution)/shard_map/ppermute | solution.py:189
  32.8 2.0 %collective-permute-start.14 = (bf16[4,48,128]{2,1,0:T(8,128)(2,1)S(1)}, bf16[4,48,128]{2,1,0:T(8,128)(2,1)S(1)}, u32[]{:S(2)}, u32[]{:S(2)}) collective-permute-start(bf16[4,48,128]{2,1,0:T(8,128)(2,1)S(1)} %get-tuple-element.44), channel_id=1, source_target_pairs={{0,24},{4,28},{8,16},{12,20},{16,8},{20,12},{24,0},{28,4},{1,25},{... | collective-permute-start | bytes 147464 | tf_op jit(solution)/shard_map/ppermute | solution.py:186
  35.1 2.3 %collective-permute-done.13.refs_3_ = bf16[4,48,128]{2,1,0:T(8,128)(2,1)S(1)} collective-permute-done((bf16[4,48,128]{2,1,0:T(8,128)(2,1)S(1)}, bf16[4,48,128]{2,1,0:T(8,128)(2,1)S(1)}, u32[]{:S(2)}, u32[]{:S(2)}) %collective-permute-start.13) | collective-permute-done | bytes 49184 | tf_op jit(solution)/shard_map/ppermute | solution.py:186
  38.7 4.0 %shard_map.49 = (bf16[12,128,128]{2,1,0:T(8,128)(2,1)S(1)}, bf16[12,128,128]{2,1,0:T(8,128)(2,1)S(1)}, bf16[12,128,128]{2,1,0:T(8,128)(2,1)S(1)}, bf16[12,128,128]{2,1,0:T(8,128)(2,1)S(1)}) custom-call(bf16[4,128,128,128]{3,2,1,0:T(8,128)(2,1)S(1)} %bitcast.4, bf16[4,48,128]{2,1,0:T(8,128)(2,1)S(1)} %get-tuple-element.41.refs_1_, ...), custom_call_target="tpu_custom_call" | custom-call | flops 805306368 | bytes 1048576 | tf_op jit(solution)/shard_map/pallas_call | solution.py:24
  46.3 9.1 %collective-permute-done.9.refs_4_ = bf16[4,128,128]{2,1,0:T(8,128)(2,1)S(1)} collective-permute-done((bf16[4,128,128]{2,1,0:T(8,128)(2,1)S(1)}, bf16[4,128,128]{2,1,0:T(8,128)(2,1)S(1)}, u32[]{:S(2)}, u32[]{:S(2)}) %collective-permute-start.9) | collective-permute-done | bytes 131104 | tf_op jit(solution)/shard_map/ppermute | solution.py:189
  58.9 2.5 %collective-permute-done.16.refs_3_ = bf16[12,128,128]{2,1,0:T(8,128)(2,1)S(1)} collective-permute-done((bf16[12,128,128]{2,1,0:T(8,128)(2,1)S(1)}, bf16[12,128,128]{2,1,0:T(8,128)(2,1)S(1)}, u32[]{:S(2)}, u32[]{:S(2)}) %collective-permute-start.16) | collective-permute-done | bytes 393248 | tf_op jit(solution)/shard_map/ppermute | solution.py:189
  61.4 6.9 %collective-permute-done.17.refs_4_ = bf16[12,128,128]{2,1,0:T(8,128)(2,1)S(1)} collective-permute-done((bf16[12,128,128]{2,1,0:T(8,128)(2,1)S(1)}, bf16[12,128,128]{2,1,0:T(8,128)(2,1)S(1)}, u32[]{:S(2)}, u32[]{:S(2)}) %collective-permute-start.17) | collective-permute-done | bytes 393248 | tf_op jit(solution)/shard_map/ppermute | solution.py:189
  68.3 2.4 %collective-permute-start.18 = (bf16[20,128,128]{2,1,0:T(8,128)(2,1)S(1)}, bf16[20,128,128]{2,1,0:T(8,128)(2,1)S(1)}, u32[]{:S(2)}, u32[]{:S(2)}) collective-permute-start(bf16[20,128,128]{2,1,0:T(8,128)(2,1)S(1)} %get-tuple-element.35.refs_1_), channel_id=1, source_target_pairs={{0,28},{4,0},{8,4},{12,8},{16,12},{20,16},{24,20},{28,24},{1,29},{... | collective-permute-start | bytes 1966088 | tf_op jit(solution)/shard_map/ppermute | solution.py:183
  72.2 3.7 %collective-permute-start.26 = (bf16[12,128,128]{2,1,0:T(8,128)(2,1)S(1)}, bf16[12,128,128]{2,1,0:T(8,128)(2,1)S(1)}, u32[]{:S(2)}, u32[]{:S(2)}) collective-permute-start(bf16[12,128,128]{2,1,0:T(8,128)(2,1)S(1)} %collective-permute-done.16.refs_3_), channel_id=1, source_target_pairs={{0,28},{4,0},{8,4},{12,8},{16,12},{20,16},{24,20},{28,24},{1,29},{... | collective-permute-start | bytes 1179656 | tf_op jit(solution)/shard_map/ppermute | solution.py:183
  77.5 2.1 %collective-permute-start.20 = (bf16[20,128,128]{2,1,0:T(8,128)(2,1)S(1)}, bf16[20,128,128]{2,1,0:T(8,128)(2,1)S(1)}, u32[]{:S(2)}, u32[]{:S(2)}) collective-permute-start(bf16[20,128,128]{2,1,0:T(8,128)(2,1)S(1)} %collective-permute-done.8.refs_3_), channel_id=1, source_target_pairs={{0,28},{4,0},{8,4},{12,8},{16,12},{20,16},{24,20},{28,24},{1,29},{... | collective-permute-start | bytes 1966088 | tf_op jit(solution)/shard_map/ppermute | solution.py:183
  80.3 3.1 %collective-permute-done.26.refs_3_ = bf16[12,128,128]{2,1,0:T(8,128)(2,1)S(1)} collective-permute-done((bf16[12,128,128]{2,1,0:T(8,128)(2,1)S(1)}, bf16[12,128,128]{2,1,0:T(8,128)(2,1)S(1)}, u32[]{:S(2)}, u32[]{:S(2)}) %collective-permute-start.26) | collective-permute-done | bytes 393248 | tf_op jit(solution)/shard_map/ppermute | solution.py:183
  83.4 3.7 %collective-permute-start.22 = (bf16[8,128,128]{2,1,0:T(8,128)(2,1)S(1)}, bf16[8,128,128]{2,1,0:T(8,128)(2,1)S(1)}, u32[]{:S(2)}, u32[]{:S(2)}) collective-permute-start(bf16[8,128,128]{2,1,0:T(8,128)(2,1)S(1)} %collective-permute-done.10.refs_4_), channel_id=1, source_target_pairs={{0,28},{4,0},{8,4},{12,8},{16,12},{20,16},{24,20},{28,24},{1,29},{... | collective-permute-start | bytes 786440 | tf_op jit(solution)/shard_map/ppermute | solution.py:183
  87.1 1.6 %shard_map.50 = (bf16[12,128,512]{2,1,0:T(8,128)(2,1)S(1)}, f32[128,128]{1,0:T(8,128)S(1)}) custom-call(bf16[512,512]{1,0:T(8,128)(2,1)S(1)} %shard_map.46.refs_0_, bf16[12,128,128]{2,1,0:T(8,128)(2,1)S(1)} %get-tuple-element.45.refs_1_, bf16[12,128,128]{2,1,0:T(8,128)(2,1)S(1)} %collective-permute-done.15.refs_2_, ...), custom_call_target="tpu_custom_call" | custom-call | flops 1006632960 | bytes 1048576 | tf_op jit(solution)/shard_map/pallas_call | solution.py:24
  94.7 7.0 %collective-permute-done.20.refs_3_ = bf16[20,128,128]{2,1,0:T(8,128)(2,1)S(1)} collective-permute-done((bf16[20,128,128]{2,1,0:T(8,128)(2,1)S(1)}, bf16[20,128,128]{2,1,0:T(8,128)(2,1)S(1)}, u32[]{:S(2)}, u32[]{:S(2)}) %collective-permute-start.20) | collective-permute-done | bytes 655392 | tf_op jit(solution)/shard_map/ppermute | solution.py:183
  102.1 2.4 %collective-permute-done.22.refs_4_ = bf16[8,128,128]{2,1,0:T(8,128)(2,1)S(1)} collective-permute-done((bf16[8,128,128]{2,1,0:T(8,128)(2,1)S(1)}, bf16[8,128,128]{2,1,0:T(8,128)(2,1)S(1)}, u32[]{:S(2)}, u32[]{:S(2)}) %collective-permute-start.22) | collective-permute-done | bytes 262176 | tf_op jit(solution)/shard_map/ppermute | solution.py:183
  110.5 2.1 %collective-permute-done.29 = bf16[128,256]{1,0:T(8,128)(2,1)S(1)} collective-permute-done((bf16[128,256]{1,0:T(8,128)(2,1)S(1)}, bf16[128,256]{1,0:T(8,128)(2,1)S(1)}, u32[]{:S(2)}, u32[]{:S(2)}) %collective-permute-start.29) | collective-permute-done | bytes 65568 | tf_op jit(solution)/shard_map/ppermute | solution.py:189
  (67 shorter events, 32.7 us)
Async XLA Ops:
  0.0 11.2 %collective-permute-start.3 = (bf16[4096,128]{1,0:T(8,128)(2,1)}, bf16[4096,128]{1,0:T(8,128)(2,1)S(1)}, u32[]{:S(2)}, u32[]{:S(2)}) collective-permute-start(bf16[4096,128]{1,0:T(8,128)(2,1)} %refs_5_.1), channel_id=1, source_target_pairs={{0,4},{4,0},{8,12},{12,8},{16,20},{20,16},{24,28},{28,24},{1,5},{5... | collective-permute-start | bytes 3145736 | tf_op jit(solution)/shard_map/ppermute | solution.py:198
  0.5 5.2 %collective-permute-start = (s32[4,3]{1,0:T(4,128)}, s32[4,3]{1,0:T(4,128)S(1)}, u32[]{:S(2)}, u32[]{:S(2)}) collective-permute-start(s32[4,3]{1,0:T(4,128)} %refs_1_.1), channel_id=1, source_target_pairs={{0,8},{4,12},{8,0},{12,4},{16,24},{20,28},{24,16},{28,20},{1,9},{5... | collective-permute-start | bytes 152 | tf_op jit(solution)/shard_map/ppermute | solution.py:186
  5.6 5.6 %collective-permute-start.2 = (s32[4,3]{1,0:T(4,128)}, s32[4,3]{1,0:T(4,128)S(1)}, u32[]{:S(2)}, u32[]{:S(2)}) collective-permute-start(s32[4,3]{1,0:T(4,128)} %refs_1_.1), channel_id=1, source_target_pairs={{0,24},{4,28},{8,16},{12,20},{16,8},{20,12},{24,0},{28,4},{1,25},{... | collective-permute-start | bytes 152 | tf_op jit(solution)/shard_map/ppermute | solution.py:186
  14.3 8.9 %collective-permute-start.5 = (bf16[4,80,128]{2,1,0:T(8,128)(2,1)S(1)}, bf16[4,80,128]{2,1,0:T(8,128)(2,1)S(1)}, u32[]{:S(2)}, u32[]{:S(2)}) collective-permute-start(bf16[4,80,128]{2,1,0:T(8,128)(2,1)S(1)} %get-tuple-element.33), channel_id=1, source_target_pairs={{0,16},{4,20},{8,24},{12,28},{16,0},{20,4},{24,8},{28,12},{1,17},{... | collective-permute-start | bytes 245768 | tf_op jit(solution)/shard_map/ppermute | solution.py:186
  16.4 6.8 %collective-permute-start.6 = (bf16[4,80,128]{2,1,0:T(8,128)(2,1)S(1)}, bf16[4,80,128]{2,1,0:T(8,128)(2,1)S(1)}, u32[]{:S(2)}, u32[]{:S(2)}) collective-permute-start(bf16[4,80,128]{2,1,0:T(8,128)(2,1)S(1)} %get-tuple-element.34), channel_id=1, source_target_pairs={{0,24},{4,28},{8,16},{12,20},{16,8},{20,12},{24,0},{28,4},{1,25},{... | collective-permute-start | bytes 245768 | tf_op jit(solution)/shard_map/ppermute | solution.py:186
  27.5 29.4 %collective-permute-start.11 = (bf16[8,128,128]{2,1,0:T(8,128)(2,1)S(1)}, bf16[8,128,128]{2,1,0:T(8,128)(2,1)S(1)}, u32[]{:S(2)}, u32[]{:S(2)}) collective-permute-start(bf16[8,128,128]{2,1,0:T(8,128)(2,1)S(1)} %get-tuple-element.40), channel_id=1, source_target_pairs={{0,3},{1,2},{2,1},{3,0},{4,7},{5,6},{6,5},{7,4},{8,11},{9,10},{10,... | collective-permute-start | bytes 786440 | tf_op jit(solution)/shard_map/ppermute | solution.py:189
  30.0 27.4 %collective-permute-start.10 = (bf16[8,128,128]{2,1,0:T(8,128)(2,1)S(1)}, bf16[8,128,128]{2,1,0:T(8,128)(2,1)S(1)}, u32[]{:S(2)}, u32[]{:S(2)}) collective-permute-start(bf16[8,128,128]{2,1,0:T(8,128)(2,1)S(1)} %get-tuple-element.39), channel_id=1, source_target_pairs={{0,3},{1,2},{2,1},{3,0},{4,7},{5,6},{6,5},{7,4},{8,11},{9,10},{10,... | collective-permute-start | bytes 786440 | tf_op jit(solution)/shard_map/ppermute | solution.py:189
  31.9 5.5 %collective-permute-start.13 = (bf16[4,48,128]{2,1,0:T(8,128)(2,1)S(1)}, bf16[4,48,128]{2,1,0:T(8,128)(2,1)S(1)}, u32[]{:S(2)}, u32[]{:S(2)}) collective-permute-start(bf16[4,48,128]{2,1,0:T(8,128)(2,1)S(1)} %get-tuple-element.43), channel_id=1, source_target_pairs={{0,16},{4,20},{8,24},{12,28},{16,0},{20,4},{24,8},{28,12},{1,17},{... | collective-permute-start | bytes 147464 | tf_op jit(solution)/shard_map/ppermute | solution.py:186
  32.8 5.9 %collective-permute-start.14 = (bf16[4,48,128]{2,1,0:T(8,128)(2,1)S(1)}, bf16[4,48,128]{2,1,0:T(8,128)(2,1)S(1)}, u32[]{:S(2)}, u32[]{:S(2)}) collective-permute-start(bf16[4,48,128]{2,1,0:T(8,128)(2,1)S(1)} %get-tuple-element.44), channel_id=1, source_target_pairs={{0,24},{4,28},{8,16},{12,20},{16,8},{20,12},{24,0},{28,4},{1,25},{... | collective-permute-start | bytes 147464 | tf_op jit(solution)/shard_map/ppermute | solution.py:186
  42.8 16.1 %collective-permute-start.15 = (bf16[12,128,128]{2,1,0:T(8,128)(2,1)S(1)}, bf16[12,128,128]{2,1,0:T(8,128)(2,1)S(1)}, u32[]{:S(2)}, u32[]{:S(2)}) collective-permute-start(bf16[12,128,128]{2,1,0:T(8,128)(2,1)S(1)} %get-tuple-element.46), channel_id=1, source_target_pairs={{0,1},{1,0},{2,3},{3,2},{4,5},{5,4},{6,7},{7,6},{8,9},{9,8},{10,11... | collective-permute-start | bytes 1179656 | tf_op jit(solution)/shard_map/ppermute | solution.py:189
  44.3 11.1 %collective-permute-start.9 = (bf16[4,128,128]{2,1,0:T(8,128)(2,1)S(1)}, bf16[4,128,128]{2,1,0:T(8,128)(2,1)S(1)}, u32[]{:S(2)}, u32[]{:S(2)}) collective-permute-start(bf16[4,128,128]{2,1,0:T(8,128)(2,1)S(1)} %get-tuple-element.38), channel_id=1, source_target_pairs={{0,3},{1,2},{2,1},{3,0},{4,7},{5,6},{6,5},{7,4},{8,11},{9,10},{10,... | collective-permute-start | bytes 393224 | tf_op jit(solution)/shard_map/ppermute | solution.py:189
  45.9 15.5 %collective-permute-start.16 = (bf16[12,128,128]{2,1,0:T(8,128)(2,1)S(1)}, bf16[12,128,128]{2,1,0:T(8,128)(2,1)S(1)}, u32[]{:S(2)}, u32[]{:S(2)}) collective-permute-start(bf16[12,128,128]{2,1,0:T(8,128)(2,1)S(1)} %get-tuple-element.47), channel_id=1, source_target_pairs={{0,2},{1,3},{2,0},{3,1},{4,6},{5,7},{6,4},{7,5},{8,10},{9,11},{10,... | collective-permute-start | bytes 1179656 | tf_op jit(solution)/shard_map/ppermute | solution.py:189
  55.4 12.9 %collective-permute-start.17 = (bf16[12,128,128]{2,1,0:T(8,128)(2,1)S(1)}, bf16[12,128,128]{2,1,0:T(8,128)(2,1)S(1)}, u32[]{:S(2)}, u32[]{:S(2)}) collective-permute-start(bf16[12,128,128]{2,1,0:T(8,128)(2,1)S(1)} %get-tuple-element.48), channel_id=1, source_target_pairs={{0,3},{1,2},{2,1},{3,0},{4,7},{5,6},{6,5},{7,4},{8,11},{9,10},{10,... | collective-permute-start | bytes 1179656 | tf_op jit(solution)/shard_map/ppermute | solution.py:189
  56.8 19.1 %collective-permute-start.7 = (bf16[20,128,128]{2,1,0:T(8,128)(2,1)S(1)}, bf16[20,128,128]{2,1,0:T(8,128)(2,1)S(1)}, u32[]{:S(2)}, u32[]{:S(2)}) collective-permute-start(bf16[20,128,128]{2,1,0:T(8,128)(2,1)S(1)} %get-tuple-element.36), channel_id=1, source_target_pairs={{0,1},{1,0},{2,3},{3,2},{4,5},{5,4},{6,7},{7,6},{8,9},{9,8},{10,11... | collective-permute-start | bytes 1966088 | tf_op jit(solution)/shard_map/ppermute | solution.py:189
  57.4 20.2 %collective-permute-start.8 = (bf16[20,128,128]{2,1,0:T(8,128)(2,1)S(1)}, bf16[20,128,128]{2,1,0:T(8,128)(2,1)S(1)}, u32[]{:S(2)}, u32[]{:S(2)}) collective-permute-start(bf16[20,128,128]{2,1,0:T(8,128)(2,1)S(1)} %get-tuple-element.37), channel_id=1, source_target_pairs={{0,2},{1,3},{2,0},{3,1},{4,6},{5,7},{6,4},{7,5},{8,10},{9,11},{10,... | collective-permute-start | bytes 1966088 | tf_op jit(solution)/shard_map/ppermute | solution.py:189
  58.9 9.4 %collective-permute-start.24 = (bf16[12,128,128]{2,1,0:T(8,128)(2,1)S(1)}, bf16[12,128,128]{2,1,0:T(8,128)(2,1)S(1)}, u32[]{:S(2)}, u32[]{:S(2)}) collective-permute-start(bf16[12,128,128]{2,1,0:T(8,128)(2,1)S(1)} %get-tuple-element.45.refs_1_), channel_id=1, source_target_pairs={{0,28},{4,0},{8,4},{12,8},{16,12},{20,16},{24,20},{28,24},{1,29},{... | collective-permute-start | bytes 1179656 | tf_op jit(solution)/shard_map/ppermute | solution.py:183
  61.4 16.1 %collective-permute-start.25 = (bf16[12,128,128]{2,1,0:T(8,128)(2,1)S(1)}, bf16[12,128,128]{2,1,0:T(8,128)(2,1)S(1)}, u32[]{:S(2)}, u32[]{:S(2)}) collective-permute-start(bf16[12,128,128]{2,1,0:T(8,128)(2,1)S(1)} %collective-permute-done.15.refs_2_), channel_id=1, source_target_pairs={{0,28},{4,0},{8,4},{12,8},{16,12},{20,16},{24,20},{28,24},{1,29},{... | collective-permute-start | bytes 1179656 | tf_op jit(solution)/shard_map/ppermute | solution.py:183
  68.3 25.6 %collective-permute-start.18 = (bf16[20,128,128]{2,1,0:T(8,128)(2,1)S(1)}, bf16[20,128,128]{2,1,0:T(8,128)(2,1)S(1)}, u32[]{:S(2)}, u32[]{:S(2)}) collective-permute-start(bf16[20,128,128]{2,1,0:T(8,128)(2,1)S(1)} %get-tuple-element.35.refs_1_), channel_id=1, source_target_pairs={{0,28},{4,0},{8,4},{12,8},{16,12},{20,16},{24,20},{28,24},{1,29},{... | collective-permute-start | bytes 1966088 | tf_op jit(solution)/shard_map/ppermute | solution.py:183
  72.2 11.2 %collective-permute-start.26 = (bf16[12,128,128]{2,1,0:T(8,128)(2,1)S(1)}, bf16[12,128,128]{2,1,0:T(8,128)(2,1)S(1)}, u32[]{:S(2)}, u32[]{:S(2)}) collective-permute-start(bf16[12,128,128]{2,1,0:T(8,128)(2,1)S(1)} %collective-permute-done.16.refs_3_), channel_id=1, source_target_pairs={{0,28},{4,0},{8,4},{12,8},{16,12},{20,16},{24,20},{28,24},{1,29},{... | collective-permute-start | bytes 1179656 | tf_op jit(solution)/shard_map/ppermute | solution.py:183
  75.9 14.1 %collective-permute-start.27 = (bf16[12,128,128]{2,1,0:T(8,128)(2,1)S(1)}, bf16[12,128,128]{2,1,0:T(8,128)(2,1)S(1)}, u32[]{:S(2)}, u32[]{:S(2)}) collective-permute-start(bf16[12,128,128]{2,1,0:T(8,128)(2,1)S(1)} %collective-permute-done.17.refs_4_), channel_id=1, source_target_pairs={{0,28},{4,0},{8,4},{12,8},{16,12},{20,16},{24,20},{28,24},{1,29},{... | collective-permute-start | bytes 1179656 | tf_op jit(solution)/shard_map/ppermute | solution.py:183
  77.5 17.1 %collective-permute-start.19 = (bf16[20,128,128]{2,1,0:T(8,128)(2,1)S(1)}, bf16[20,128,128]{2,1,0:T(8,128)(2,1)S(1)}, u32[]{:S(2)}, u32[]{:S(2)}) collective-permute-start(bf16[20,128,128]{2,1,0:T(8,128)(2,1)S(1)} %collective-permute-done.7.refs_2_), channel_id=1, source_target_pairs={{0,28},{4,0},{8,4},{12,8},{16,12},{20,16},{24,20},{28,24},{1,29},{... | collective-permute-start | bytes 1966088 | tf_op jit(solution)/shard_map/ppermute | solution.py:183
  77.5 24.1 %collective-permute-start.20 = (bf16[20,128,128]{2,1,0:T(8,128)(2,1)S(1)}, bf16[20,128,128]{2,1,0:T(8,128)(2,1)S(1)}, u32[]{:S(2)}, u32[]{:S(2)}) collective-permute-start(bf16[20,128,128]{2,1,0:T(8,128)(2,1)S(1)} %collective-permute-done.8.refs_3_), channel_id=1, source_target_pairs={{0,28},{4,0},{8,4},{12,8},{16,12},{20,16},{24,20},{28,24},{1,29},{... | collective-permute-start | bytes 1966088 | tf_op jit(solution)/shard_map/ppermute | solution.py:183
  83.4 21.1 %collective-permute-start.22 = (bf16[8,128,128]{2,1,0:T(8,128)(2,1)S(1)}, bf16[8,128,128]{2,1,0:T(8,128)(2,1)S(1)}, u32[]{:S(2)}, u32[]{:S(2)}) collective-permute-start(bf16[8,128,128]{2,1,0:T(8,128)(2,1)S(1)} %collective-permute-done.10.refs_4_), channel_id=1, source_target_pairs={{0,28},{4,0},{8,4},{12,8},{16,12},{20,16},{24,20},{28,24},{1,29},{... | collective-permute-start | bytes 786440 | tf_op jit(solution)/shard_map/ppermute | solution.py:183
  90.0 15.9 %collective-permute-start.21 = (bf16[4,128,128]{2,1,0:T(8,128)(2,1)S(1)}, bf16[4,128,128]{2,1,0:T(8,128)(2,1)S(1)}, u32[]{:S(2)}, u32[]{:S(2)}) collective-permute-start(bf16[4,128,128]{2,1,0:T(8,128)(2,1)S(1)} %collective-permute-done.9.refs_4_), channel_id=1, source_target_pairs={{0,28},{4,0},{8,4},{12,8},{16,12},{20,16},{24,20},{28,24},{1,29},{... | collective-permute-start | bytes 393224 | tf_op jit(solution)/shard_map/ppermute | solution.py:183
  (14 other events, 160.4 us)
